TPU v7x, 128 devices: a whole 4x4x4 slice. The times are simulated.
128 devices in a mesh: group: 16 (over z, x_hi, core), tensor: 8 (over x_lo, y).
Axes of the slice: x: 4 (x_hi: 2, x_lo: 2; x = x_hi * 2 + x_lo), y: 4, z: 4, core: 2. Of those that a mesh axis runs over, the one named last changes fastest.
Arguments:
- hidden_in: bfloat16 [4096, 4096], P(('group', 'tensor')), may hold values from -6 to 6
- queries: bfloat16 [4096, 4096], P('group', 'tensor'), may hold values from -72 to 72
- new_kv: bfloat16 [2, 4096, 1024], P(None, 'group', 'tensor'), may hold values from -6 to 6
- pool_codes: bfloat16 [2, 32768, 1024], P(None, 'group', 'tensor'), may hold values from -1 to 1
- pool_scales: float32 [2, 64, 8], P(None, 'group', 'tensor'), may hold values from 0.5 to 4
- block_table: int32 [16, 16], replicated, may hold values from 0 to 63, as said below
- prefix_blocks: int32 [16], replicated, may hold values from 8 to 16, as said below
- out_proj: bfloat16 [4096, 4096], P('tensor'), may hold values from -0.09375 to 0.09375
- norm_gain: float32 [4096], replicated, may hold values from 0.5 to 1.5
- expert_ids: int32 [4096, 2], P(('group', 'tensor')), may hold values from 0 to 7, all different within a row; in each aligned block of 32 rows (0 to 31, 32 to 63, ...) at most 12 rows name the same one
- expert_share: float32 [4096], P(('group', 'tensor')), may hold values from 0.1 to 0.9
- gate_proj: bfloat16 [8, 8192, 4096], P('tensor', 'group'), may hold values from -0.09375 to 0.09375
- up_proj: bfloat16 [8, 8192, 4096], P('tensor', 'group'), may hold values from -0.09375 to 0.09375
- down_proj: bfloat16 [8, 8192, 4096], P('tensor', 'group'), may hold values from -0.0625 to 0.0625
- new_slots: int32 [32], replicated, may hold values from 0 to 31, as said below
Outputs:
- layer_out: bfloat16 [4096, 4096], P(('group', 'tensor'))
- new_codes: bfloat16 [2, 4096, 1024], P(None, 'group', 'tensor')
- new_scales: bfloat16 [2, 32, 8], P(None, 'group', 'tensor')
Inputs may be any that keep to these rules, and one draw needn't show every extreme that they name: `block_table`: an entry b is block b % 4 of owner group b // 4. The 16 entries of a group's row lie on 16 different owners; several groups may share the same blocks. A group's prefix is the first prefix_blocks[g] entries of its row. `expert_ids`: within the 32 rows of one device no expert is named by more than 12 rows. A permutation: the block of sequence q (q // 2 its group) goes to owner group new_slots[q] // 2; the 2 sequences of one group go to different owners.
All inputs are finite; a program needn't handle non-finite values. Where the computation divides by a largest or mean magnitude, that divisor is 1e-20 or more.
Results may differ from a plain program's by a relative error of at most 0.0095.
Values may be sent and summed in bfloat16 or wider, within the bound.
No kernel may reach another device: no remote copies, remote signals or barrier semaphores. Data moves between devices by JAX's collectives and lax.ppermute only.
A program may use at most 128 MiB of HBM per device.

v0:
```python
import functools
import math

import jax
import jax.numpy as jnp
from jax import lax
from jax.experimental import pallas as pl
from jax.experimental.pallas import tpu as pltpu
from jax.sharding import Mesh
from jax.sharding import PartitionSpec as P


EXPERTS = 8
TOP = 2
SUFFIX = 128
CAP = 12
GROUP = ("z", "xh", "c")
TENSOR = ("xl", "y")
SPLIT = 2048
PER = 4


def shift_z(x, by):
    n = lax.axis_size("z")
    return lax.ppermute(x, "z", [(i, (i + by) % n) for i in range(n)])


def swap(x, axis):
    return lax.ppermute(x, axis, [(0, 1), (1, 0)])


def plus(*terms):
    return sum(t.astype(jnp.float32) for t in terms)


def select_body(picked, scale_ref, codes_ref, *refs):
    outs, (pool_sc, sem) = refs[:-2], refs[-2:]
    pool = codes_ref.shape[1]
    for b in range(pool):
        for c in range(2):
            s = scale_ref[c, b, 0]
            pool_sc[b, c] = (codes_ref[c, b].astype(jnp.float32) * s).astype(jnp.bfloat16)
    copies, row = [], 0
    for i, out in enumerate(outs):
        rows = out.shape[2]
        for g in range(out.shape[0]):
            src = pool_sc.at[picked[g], :, pl.ds(row, rows)]
            copies.append(pltpu.make_async_copy(src, out.at[g], sem.at[i, g]))
        row += rows
    for copy in copies:
        copy.start()
    for copy in copies:
        copy.wait()


def select_blocks(picked, scales, codes, cuts):
    _, pool, rows, width = codes.shape
    groups = picked.shape[0]
    return pl.pallas_call(
        select_body,
        grid_spec=pltpu.PrefetchScalarGridSpec(
            num_scalar_prefetch=1,
            grid=(1,),
            in_specs=[
                pl.BlockSpec(memory_space=pltpu.SMEM),
                pl.BlockSpec(codes.shape, lambda i, p: (0, 0, 0, 0)),
            ],
            out_specs=[pl.BlockSpec(memory_space=pl.ANY)] * len(cuts),
            scratch_shapes=[
                pltpu.VMEM((pool, 2, rows, width), jnp.bfloat16),
                pltpu.SemaphoreType.DMA((len(cuts), groups)),
            ],
        ),
        out_shape=[jax.ShapeDtypeStruct((groups, 2, n, width), jnp.bfloat16) for n in cuts],
        cost_estimate=pl.CostEstimate(flops=1 << 20, bytes_accessed=6 << 20, transcendentals=0),
        name="select",
    )(picked, scales, codes)


def attend_body(begin, end, per, live, q_ref, new_ref, kv_ref, *refs):
    state, refs = (None, refs) if begin else (refs[:2], refs[2:])
    outs, refs = (refs[:1], refs[1:]) if end else (refs[:2], refs[2:])
    m_sc, acc_sc = refs[:2] if end else outs
    q_sc, v_sc = refs[-2:]
    step = pl.program_id(0)
    toks, dim = q_ref.shape[0], new_ref.shape[2]
    keys = kv_ref.shape[2]
    heads = q_ref.shape[1] // dim
    factor = math.log2(math.e) / math.sqrt(dim)
    nt = (((1,), (1,)), ((), ()))

    @pl.when(step == 0)
    def _():
        v_sc[:, dim:] = jnp.ones((v_sc.shape[0], dim), jnp.bfloat16)
        for h in range(heads):
            q_sc[h * toks : (h + 1) * toks] = q_ref[:, h * dim : (h + 1) * dim]
        if begin:
            v_sc[:toks, :dim] = new_ref[1]
            tok = lax.broadcasted_iota(jnp.int32, (toks, toks), 0)
            key = lax.broadcasted_iota(jnp.int32, (toks, toks), 1)
            seen = jnp.logical_and(tok // SUFFIX == key // SUFFIX, key <= tok)
            for h in range(heads):
                rows = slice(h * toks, (h + 1) * toks)
                s = lax.dot_general(q_sc[rows], new_ref[0], nt, preferred_element_type=jnp.float32)
                s = jnp.where(seen, s * factor, -1e30)
                m = jnp.max(s, axis=1, keepdims=True)
                p = jnp.exp2(s - m).astype(jnp.bfloat16)
                m_sc[rows] = jnp.broadcast_to(m, (toks, dim))
                acc_sc[rows] = jnp.dot(p, v_sc[:toks], preferred_element_type=jnp.float32)
        else:
            m_sc[...] = state[0][...]
            acc_sc[...] = state[1][...]

    alive = [live[step * per + i] for i in range(per)]

    @pl.when(sum(alive) > 0)
    def _():
        for i in range(per):
            v_sc[i * keys : (i + 1) * keys, :dim] = kv_ref[i, 1]
        k = kv_ref[:, 0].reshape(per * keys, dim)
        if per > 1:
            part = lax.broadcasted_iota(jnp.int32, (1, per * keys), 1) // keys
            hide = jnp.zeros((1, per * keys), jnp.float32)
            for i in range(per):
                gone = jnp.where(alive[i] > 0, 0.0, -1e30).astype(jnp.float32)
                hide = jnp.where(part == i, gone, hide)
        for h in range(heads):
            rows = slice(h * toks, (h + 1) * toks)
            s = lax.dot_general(q_sc[rows], k, nt, preferred_element_type=jnp.float32) * factor
            if per > 1:
                s = s + hide
            old = m_sc[rows][:, :1]
            m = jnp.maximum(old, jnp.max(s, axis=1, keepdims=True))
            p = jnp.exp2(s - m).astype(jnp.bfloat16)
            m_sc[rows] = jnp.broadcast_to(m, (toks, dim))
            acc_sc[rows] = acc_sc[rows] * jnp.exp2(old - m) + jnp.dot(
                p, v_sc[: per * keys], preferred_element_type=jnp.float32
            )

    if end:

        @pl.when(step == pl.num_programs(0) - 1)
        def _():
            for h in range(heads):
                rows = slice(h * toks, (h + 1) * toks)
                outs[0][:, h * dim : (h + 1) * dim] = (
                    acc_sc[rows][:, :dim] / acc_sc[rows][:, dim:]
                ).astype(jnp.bfloat16)


def attention(live, queries, new_kv, got, state, end, per):
    owners, _, rows, dim = got.shape
    toks, width = queries.shape
    whole = lambda shape: pl.BlockSpec(shape, lambda i, p: (0,) * len(shape))
    total = width // dim * toks
    begin = state is None
    carried = [
        jax.ShapeDtypeStruct((total, dim), jnp.float32),
        jax.ShapeDtypeStruct((total, 2 * dim), jnp.float32),
    ]
    results = [jax.ShapeDtypeStruct(queries.shape, jnp.bfloat16)] if end else carried
    return pl.pallas_call(
        functools.partial(attend_body, begin, end, per),
        grid_spec=pltpu.PrefetchScalarGridSpec(
            num_scalar_prefetch=1,
            grid=(owners // per,),
            in_specs=[
                whole(queries.shape),
                whole(new_kv.shape),
                pl.BlockSpec((per, 2, rows, dim), lambda i, p: (i, 0, 0, 0)),
            ]
            + ([] if begin else [whole(c.shape) for c in carried]),
            out_specs=[whole(r.shape) for r in results],
            scratch_shapes=([pltpu.VMEM(c.shape, c.dtype) for c in carried] if end else [])
            + [
                pltpu.VMEM((total, dim), jnp.bfloat16),
                pltpu.VMEM((max(per * rows, toks) if begin else per * rows, 2 * dim), jnp.bfloat16),
            ],
        ),
        out_shape=results,
        cost_estimate=pl.CostEstimate(
            flops=6 * total * rows * dim * owners,
            bytes_accessed=5 << 20,
            transcendentals=total * rows * owners,
        ),
        name="attend",
    )(live, queries, new_kv, got, *(() if begin else state))


def store_body(pick, *refs):
    ins, (codes_ref, scale_ref) = refs[:-2], refs[-2:]
    at = pick[3 * pl.program_id(0)]
    for c in range(2):
        x = ins[0][0, c]
        for i in range(1, len(ins)):
            x = jnp.where(at == i, ins[i][0, c], x)
        x = x.astype(jnp.float32)
        top = jnp.max(jnp.max(jnp.abs(x), axis=0, keepdims=True), axis=1, keepdims=True)
        scale = (top + 1e-06).astype(jnp.bfloat16).astype(jnp.float32)
        codes_ref[c] = (x / scale).astype(jnp.bfloat16)
        scale_ref[0, c : c + 1] = jnp.broadcast_to(scale, (1, scale_ref.shape[2]))


def store_blocks(pick, gathered, seqs):
    _, _, _, dim = gathered[0].shape
    source = pl.BlockSpec((1, 2, SUFFIX, dim), lambda k, p: (p[3 * k + 1], 0, p[3 * k + 2], 0))
    return pl.pallas_call(
        store_body,
        grid_spec=pltpu.PrefetchScalarGridSpec(
            num_scalar_prefetch=1,
            grid=(seqs,),
            in_specs=[source] * len(gathered),
            out_specs=[
                pl.BlockSpec((2, SUFFIX, dim), lambda k, p: (0, k, 0)),
                pl.BlockSpec((1, 2, dim), lambda k, p: (k, 0, 0)),
            ],
        ),
        out_shape=[
            jax.ShapeDtypeStruct((2, seqs * SUFFIX, dim), jnp.bfloat16),
            jax.ShapeDtypeStruct((seqs, 2, dim), jnp.float32),
        ],
        cost_estimate=pl.CostEstimate(flops=1 << 17, bytes_accessed=1 << 18, transcendentals=0),
        name="store",
    )(pick, *gathered)


def hidden_body(moves, *refs):
    n_in = len(moves)
    ins, refs = refs[:n_in], refs[n_in:]
    own, other, (out_ref, x_sc, sem) = refs[:2], refs[2:4], refs[4:]
    step, steps = pl.program_id(0), pl.num_programs(0)
    nt = (((1,), (1,)), ((), ()))

    @pl.when(step == 0)
    def _():
        copies = []
        for i, (ref, (r, c)) in enumerate(zip(ins, moves)):
            dst = x_sc.at[pl.ds(r, ref.shape[0]), pl.ds(c, ref.shape[1])]
            copies.append(pltpu.make_async_copy(ref, dst, sem.at[i]))
        for copy in copies:
            copy.start()
        for copy in copies:
            copy.wait()

    def run(gate, up):
        x = x_sc[...]
        g = lax.dot_general(x, gate[0], nt, preferred_element_type=jnp.float32)
        u = lax.dot_general(x, up[0], nt, preferred_element_type=jnp.float32)
        out_ref[...] = (g / (1.0 + jnp.exp(-g)) * u).astype(jnp.bfloat16)

    @pl.when(step < steps // 2)
    def _():
        run(*own)

    @pl.when(step >= steps // 2)
    def _():
        run(*other)


def hidden_units(pieces, own, other, rows, tile=256):
    _, units, width = own[0].shape
    half = units // tile
    first = pl.BlockSpec((1, tile, width), lambda i: (0, jnp.minimum(i, half - 1), 0))
    second = pl.BlockSpec((1, tile, width), lambda i: (0, jnp.maximum(i - half, 0), 0))
    ins, moves = zip(*pieces)
    return pl.pallas_call(
        functools.partial(hidden_body, moves),
        grid=(2 * half,),
        in_specs=[pl.BlockSpec(memory_space=pl.ANY)] * len(ins) + [first] * 2 + [second] * 2,
        out_specs=pl.BlockSpec((rows, tile), lambda i: (0, i)),
        out_shape=jax.ShapeDtypeStruct((rows, 2 * units), jnp.bfloat16),
        scratch_shapes=[
            pltpu.VMEM((rows, width), jnp.bfloat16),
            pltpu.SemaphoreType.DMA((len(ins),)),
        ],
        compiler_params=pltpu.CompilerParams(vmem_limit_bytes=56_000_000),
        cost_estimate=pl.CostEstimate(
            flops=8 * rows * units * width,
            bytes_accessed=8 * units * width + 2 * rows * width,
            transcendentals=2 * rows * units,
        ),
        name="hidden",
    )(*ins, *own[:2], *other[:2])


def down_body(moves, n_in, *refs):
    ins, (own, other), outs = refs[:n_in], refs[n_in : n_in + 2], refs[n_in + 2 :]
    units = own.shape[1]
    for of, ref in enumerate(ins):
        h = ref[...]
        y = jnp.dot(h[:, :units], own[0], preferred_element_type=jnp.float32)
        y += jnp.dot(h[:, units:], other[0], preferred_element_type=jnp.float32)
        y = y.astype(jnp.bfloat16)
        for out, places in zip(outs, moves):
            n = out.shape[0] // len(places)
            for i, (source, r) in enumerate(places):
                if source == of:
                    out[i * n : (i + 1) * n] = y[r : r + n]


def down_sums(hidden, own, other, start, size, shapes_out, tile=512):
    _, units, _ = own[2].shape
    weight = pl.BlockSpec((1, units, tile), lambda i: (0, 0, start // tile + i))
    rows, moves = zip(*shapes_out)
    total = sum(h.shape[0] for h in hidden)
    return pl.pallas_call(
        functools.partial(down_body, moves, len(hidden)),
        grid=(size // tile,),
        in_specs=[pl.BlockSpec(h.shape, lambda i: (0, 0)) for h in hidden] + [weight, weight],
        out_specs=[pl.BlockSpec((n, tile), lambda i: (0, i)) for n in rows],
        out_shape=[jax.ShapeDtypeStruct((n, size), jnp.bfloat16) for n in rows],
        compiler_params=pltpu.CompilerParams(vmem_limit_bytes=40_000_000),
        cost_estimate=pl.CostEstimate(
            flops=4 * total * units * size,
            bytes_accessed=4 * units * size + 2 * total * size + 4 * total * units,
            transcendentals=0,
        ),
        name="down",
    )(*hidden, own[2], other[2])


def local(
    hidden_in,
    queries,
    new_kv,
    pool_codes,
    pool_scales,
    block_table,
    prefix_blocks,
    out_proj,
    norm_gain,
    expert_ids,
    expert_share,
    gate_proj,
    up_proj,
    down_proj,
    new_slots,
):
    groups = lax.axis_size(GROUP)
    tensors = lax.axis_size(TENSOR)
    n_z = lax.axis_size("z")
    my_group = lax.axis_index(GROUP)
    pool = pool_scales.shape[1]
    dim = pool_codes.shape[2]
    pblock = pool_codes.shape[1] // pool
    group_tok = queries.shape[0]
    seqs = group_tok // SUFFIX
    model_width = hidden_in.shape[1]

    owners = block_table // pool
    position = lax.broadcasted_iota(jnp.int32, block_table.shape, 1)
    mine = jnp.logical_and(owners == my_group, position < prefix_blocks[:, None])
    picked = jnp.sum(jnp.where(mine, block_table % pool, 0), axis=1)
    (outgoing,) = select_blocks(
        picked, pool_scales, pool_codes.reshape(2, pool, pblock, dim), (pblock,)
    )
    got = lax.all_to_all(outgoing, GROUP, split_axis=0, concat_axis=0, tiled=True)
    my_row = lax.dynamic_index_in_dim(block_table, my_group, 0, keepdims=False)
    my_length = lax.dynamic_index_in_dim(prefix_blocks, my_group, 0, keepdims=False)
    row_live = lax.broadcasted_iota(jnp.int32, my_row.shape, 0) < my_length
    owner_iota = lax.broadcasted_iota(jnp.int32, (groups, my_row.shape[0]), 0)
    live = jnp.any(
        jnp.logical_and((my_row // pool)[None, :] == owner_iota, row_live[None, :]), axis=1
    ).astype(jnp.int32)

    fresh = jnp.stack([new_kv, swap(new_kv, "c")])
    fresh = jnp.concatenate([fresh, swap(fresh, "xh")])
    own = (gate_proj, up_proj, down_proj)
    own_late, got = lax.optimization_barrier((own, got))
    other = []
    for w in own_late:
        other.append(swap(w, "c"))

    (attn,) = attention(live, queries, new_kv, got, None, True, PER)
    partial = jnp.dot(attn, out_proj, preferred_element_type=jnp.float32).astype(jnp.bfloat16)
    partial = partial.reshape(tensors, group_tok // tensors, model_width)
    arrived = lax.all_to_all(partial, TENSOR, split_axis=0, concat_axis=0, tiled=True)
    gathered = [fresh]
    for k in range(1, n_z):
        gathered.append(shift_z(fresh, k))
    resid = hidden_in.astype(jnp.float32) + arrived.astype(jnp.float32).sum(axis=0)
    normed = (
        resid * lax.rsqrt(jnp.mean(resid * resid, axis=1, keepdims=True) + 1e-05) * norm_gain
    ).astype(jnp.bfloat16)

    tok_dev = group_tok // tensors
    pair_ids = expert_ids.reshape(-1)
    onehot = (
        pair_ids[:, None] == lax.broadcasted_iota(jnp.int32, (pair_ids.shape[0], EXPERTS), 1)
    ).astype(jnp.int32)
    rank = jnp.sum(onehot * (jnp.cumsum(onehot, axis=0) - 1), axis=1)
    slot = (pair_ids * CAP + rank).reshape(tok_dev, TOP)
    slot_iota = lax.broadcasted_iota(jnp.int32, (EXPERTS * CAP,), 0)
    matches = slot[:, :, None] == slot_iota[None, None, :]
    route_rows = jnp.any(matches, axis=1).astype(jnp.bfloat16)
    pair_weight = jnp.stack([expert_share, 1.0 - expert_share], axis=1)
    combine = jnp.sum(jnp.where(matches, pair_weight[:, :, None], 0.0), axis=1)
    outbound = jnp.einsum(
        "ie,id->ed", route_rows, normed, preferred_element_type=jnp.float32
    ).astype(jnp.bfloat16)
    landed = lax.all_to_all(outbound, TENSOR, split_axis=0, concat_axis=0, tiled=True)

    n = landed.shape[0]
    a, b = landed[:, :SPLIT], landed[:, SPLIT:]
    wide = model_width - SPLIT
    half = wide // 2
    ax = swap(a, "xh")
    b_r = shift_z(b, 1)
    b_l = shift_z(b, -1)
    bx = swap(b, "xh")
    a2 = jnp.concatenate([a, ax])
    a_r = shift_z(a2, 1)
    a_l = shift_z(a2, -1)
    bx_rl = swap(jnp.concatenate([b_r, b_l]), "xh")
    b_f1 = shift_z(b_r[:, :half], 1)
    b_f2 = shift_z(b_l[:, half:], -1)
    bx_f = swap(jnp.concatenate([b_f1, b_f2], axis=1), "xh")
    a_f1 = shift_z(a_r[:n], 1)
    a_f2 = shift_z(a_l[n:], -1)

    A, B = SPLIT, wide
    h_o = hidden_units([(a2, (0, 0)), (b, (0, A)), (bx, (n, A))], own, other, 2 * n)
    h_r = hidden_units(
        [(a_r, (0, 0)), (a_l, (2 * n, 0)), (a_f1, (4 * n, 0)), (a_f2, (5 * n, 0))]
        + [(b_r, (0, A)), (b_l, (2 * n, A))]
        + [(bx_rl[:n], (n, A)), (bx_rl[n:], (3 * n, A))]
        + [(b_f1, (4 * n, A)), (b_f2, (4 * n, A + half)), (bx_f, (5 * n, A))],
        own,
        other,
        6 * n,
    )
    o_b, r_b, l_b, f_b, x_o, x_rl, x_f = down_sums(
        [h_o, h_r],
        own,
        other,
        A,
        B,
        [(n, ((0, 0),)), (n, ((1, 0),)), (n, ((1, 2 * n),)), (n, ((1, 4 * n),))]
        + [(n, ((0, n),)), (2 * n, ((1, n), (1, 3 * n))), (n, ((1, 5 * n),))],
    )
    o_a, r_a, l_a, f1_a, f2_a = down_sums(
        [h_o, h_r],
        own,
        other,
        0,
        A,
        [(2 * n, ((0, 0),)), (2 * n, ((1, 0),)), (2 * n, ((1, 2 * n),))]
        + [(n, ((1, 4 * n),)), (n, ((1, 5 * n),))],
    )

    bf = jnp.bfloat16
    u_o = swap(x_o, "xh")
    u_rl = swap(x_rl, "xh")
    u_f = swap(x_f, "xh")
    back1 = shift_z(f1_a, -1)
    back2 = shift_z(f2_a, 1)
    r_a = jnp.concatenate([plus(r_a[:n], back1), plus(r_a[n:])]).astype(bf)
    l_a = jnp.concatenate([plus(l_a[:n]), plus(l_a[n:], back2)]).astype(bf)
    t_r = shift_z(r_a, -1)
    t_l = shift_z(l_a, 1)
    s_a = plus(o_a, t_r, t_l)
    t_x = swap(s_a[n:].astype(bf), "xh")
    part_a = plus(s_a[:n], t_x)
    f_b = plus(f_b, u_f).astype(bf)
    v1 = shift_z(f_b[:, :half], -1)
    v2 = shift_z(f_b[:, half:], 1)
    r_b, l_b = plus(r_b, u_rl[:n]), plus(l_b, u_rl[n:])
    r_b = jnp.concatenate([plus(r_b[:, :half], v1), r_b[:, half:]], axis=1).astype(bf)
    l_b = jnp.concatenate([l_b[:, :half], plus(l_b[:, half:], v2)], axis=1).astype(bf)
    v_r = shift_z(r_b, -1)
    v_l = shift_z(l_b, 1)
    part_b = plus(o_b, u_o, v_r, v_l)
    summed = jnp.concatenate([part_a, part_b], axis=1).astype(bf)
    returned = lax.all_to_all(summed, TENSOR, split_axis=0, concat_axis=0, tiled=True)
    mixture = jnp.dot(
        combine,
        returned.astype(jnp.float32),
        precision=lax.Precision.HIGHEST,
        preferred_element_type=jnp.float32,
    )
    layer_out = (resid + mixture).astype(jnp.bfloat16)

    wanted = my_group * seqs + lax.broadcasted_iota(jnp.int32, (seqs, 1), 0)
    seq_iota = lax.broadcasted_iota(jnp.int32, (seqs, new_slots.shape[0]), 1)
    source = jnp.sum(jnp.where(new_slots[None, :] == wanted, seq_iota, 0), axis=1)
    from_group = source // seqs
    dz = (lax.axis_index("z") - from_group // 4) % n_z
    dx = (from_group // 2 % 2) ^ lax.axis_index("xh")
    dc = (from_group % 2) ^ lax.axis_index("c")
    pick = jnp.stack([dz, dx * 2 + dc, source % seqs], axis=1).reshape(-1).astype(jnp.int32)
    new_codes, scales = store_blocks(pick, gathered, seqs)
    new_scales = jnp.swapaxes(scales[:, :, :1], 0, 1).astype(jnp.bfloat16)
    return (layer_out, new_codes, new_scales)


def solution(mesh):
    fine = Mesh(mesh.devices.reshape(4, 2, 2, 2, 4), GROUP + TENSOR)
    placed = (
        P(GROUP + TENSOR, None),
        P(GROUP, TENSOR),
        P(None, GROUP, TENSOR),
        P(None, GROUP, TENSOR),
        P(None, GROUP, TENSOR),
        P(),
        P(),
        P(TENSOR, None),
        P(),
        P(GROUP + TENSOR, None),
        P(GROUP + TENSOR),
        P(TENSOR, GROUP, None),
        P(TENSOR, GROUP, None),
        P(TENSOR, GROUP, None),
        P(),
    )
    return jax.shard_map(
        local,
        mesh=fine,
        in_specs=placed,
        out_specs=(
            P(GROUP + TENSOR, None),
            P(None, GROUP, TENSOR),
            P(None, GROUP, TENSOR),
        ),
        check_vma=False,
    )
```

profile of v0, /device:TPU:0, one launch (start us, length us, event | category | flops | bytes accessed | tf_op | source)
XLA Modules:
  0.0 347.6 jit_solution(17668112897285683629)
XLA Ops:
  3.4 4.2 %select.148 = bf16[16,2,512,128]{3,2,1,0:T(8,128)(2,1)} custom-call(s32[16]{0:T(128)} %fusion.10.picked, f32[2,4,1]{2,1,0:T(4,128)} %copy.39.scale_ref, bf16[2,4,512,128]{3,2,1,0:T(8,128)(2,1)} %bitcast.37), custom_call_target="tpu_custom_call" | custom-call | flops 1048576 | bytes 6291456 | tf_op jit(solution)/shard_map/select/pallas_call | solution.py:59
  7.6 8.1 %all-to-all-start = ((bf16[16,2,512,128]{3,2,1,0:T(8,128)(2,1)}), bf16[16,2,512,128]{3,2,1,0:T(8,128)(2,1)}, u32[]{:S(2)}, u32[]{:S(2)}) async-start(bf16[16,2,512,128]{3,2,1,0:T(8,128)(2,1)} %select.148), calls=%async_computation | async-start | bytes 8388608 | tf_op jit(solution)/shard_map/all_to_all | solution.py:357
  18.3 49.2 %all-to-all-done.kv_ref = bf16[16,2,512,128]{3,2,1,0:T(8,128)(2,1)} async-done(((bf16[16,2,512,128]{3,2,1,0:T(8,128)(2,1)}), bf16[16,2,512,128]{3,2,1,0:T(8,128)(2,1)}, u32[]{:S(2)}, u32[]{:S(2)}) %all-to-all-start) | async-done | bytes 4194336 | tf_op jit(solution)/shard_map/all_to_all | solution.py:357
  67.5 17.5 %attend.1 = bf16[256,512]{1,0:T(8,128)(2,1)} custom-call(s32[16]{0:T(128)} %convert_element_type.103.live, bf16[256,512]{1,0:T(8,128)(2,1)} %q_ref.1, bf16[2,256,128]{2,1,0:T(8,128)(2,1)} %new_ref.1, bf16[16,2,512,128]{3,2,1,0:T(8,128)(2,1)} %all-to-all-done.kv_ref), custom_call_target="tpu_custom_call" | custom-call | flops 6442450944 | bytes 5242880 | tf_op jit(solution)/shard_map/attend/pallas_call | solution.py:162
  85.0 4.9 %convolution_convert_fusion = bf16[256,4096]{1,0:T(8,128)(2,1)} fusion(bf16[256,512]{1,0:T(8,128)(2,1)} %attend.1, bf16[512,4096]{1,0:T(8,128)(2,1)} %param.22), kind=kOutput, calls=%fused_computation | convolution fusion | flops 1074790400 | bytes 6553600 | tf_op jit(solution)/shard_map/dot_general | solution.py:375
  89.9 4.6 %all-to-all-start.1 = ((bf16[8,32,4096]{2,1,0:T(8,128)(2,1)}), bf16[8,32,4096]{2,1,0:T(8,128)(2,1)S(1)}, u32[]{:S(2)}, u32[]{:S(2)}) async-start(bf16[8,32,4096]{2,1,0:T(8,128)(2,1)} %bitcast.36), calls=%async_computation.1 | async-start | bytes 4194304 | tf_op jit(solution)/shard_map/all_to_all | solution.py:377
  96.0 24.2 %all-to-all-done.1 = bf16[8,32,4096]{2,1,0:T(8,128)(2,1)S(1)} async-done(((bf16[8,32,4096]{2,1,0:T(8,128)(2,1)}), bf16[8,32,4096]{2,1,0:T(8,128)(2,1)S(1)}, u32[]{:S(2)}, u32[]{:S(2)}) %all-to-all-start.1) | async-done | bytes 2097184 | tf_op jit(solution)/shard_map/all_to_all | solution.py:377
  126.0 14.9 %all-to-all-done.2 = bf16[8,12,4096]{2,1,0:T(8,128)(2,1)S(1)} async-done(((bf16[8,12,4096]{2,1,0:T(8,128)(2,1)}), bf16[8,12,4096]{2,1,0:T(8,128)(2,1)S(1)}, u32[]{:S(2)}, u32[]{:S(2)}) %all-to-all-start.2) | async-done | bytes 786464 | tf_op jit(solution)/shard_map/all_to_all | solution.py:401
  144.7 8.5 %collective-permute-done.8.refs_4_ = bf16[96,2048]{1,0:T(8,128)(2,1)S(1)} collective-permute-done((bf16[96,2048]{1,0:T(8,128)(2,1)S(1)}, bf16[96,2048]{1,0:T(8,128)(2,1)S(1)}, u32[]{:S(2)}, u32[]{:S(2)}) %collective-permute-start.8) | collective-permute-done | bytes 393248 | tf_op jit(solution)/shard_map/ppermute | solution.py:25
  156.2 6.9 %collective-permute-done.9.refs_5_ = bf16[96,2048]{1,0:T(8,128)(2,1)S(1)} collective-permute-done((bf16[96,2048]{1,0:T(8,128)(2,1)S(1)}, bf16[96,2048]{1,0:T(8,128)(2,1)S(1)}, u32[]{:S(2)}, u32[]{:S(2)}) %collective-permute-start.9) | collective-permute-done | bytes 393248 | tf_op jit(solution)/shard_map/ppermute | solution.py:25
  169.6 3.7 %collective-permute-start.5 = (bf16[192,2048]{1,0:T(8,128)(2,1)S(1)}, bf16[192,2048]{1,0:T(8,128)(2,1)}, u32[]{:S(2)}, u32[]{:S(2)}) collective-permute-start(bf16[192,2048]{1,0:T(8,128)(2,1)S(1)} %pad_maximum_fusion.1.refs_0_), channel_id=1, source_target_pairs={{0,96},{32,0},{64,32},{96,64},{1,97},{33,1},{65,33},{97,65},{2,98}... | collective-permute-start | bytes 2359304 | tf_op jit(solution)/shard_map/ppermute | solution.py:25
  173.4 8.5 %collective-permute-done.4.refs_0_ = bf16[192,2048]{1,0:T(8,128)(2,1)} collective-permute-done((bf16[192,2048]{1,0:T(8,128)(2,1)S(1)}, bf16[192,2048]{1,0:T(8,128)(2,1)}, u32[]{:S(2)}, u32[]{:S(2)}) %collective-permute-start.4) | collective-permute-done | bytes 786464 | tf_op jit(solution)/shard_map/ppermute | solution.py:25
  191.0 17.4 %collective-permute-done.1.refs_2_ = bf16[96,2048]{1,0:T(8,128)(2,1)S(1)} collective-permute-done((bf16[96,2048]{1,0:T(8,128)(2,1)S(1)}, bf16[96,2048]{1,0:T(8,128)(2,1)S(1)}, u32[]{:S(2)}, u32[]{:S(2)}) %collective-permute-start.1) | collective-permute-done | bytes 393248 | tf_op jit(solution)/shard_map/ppermute | solution.py:29
  216.2 12.3 %hidden.2.refs_0_ = bf16[192,1024]{1,0:T(8,128)(2,1)S(1)} custom-call(bf16[192,2048]{1,0:T(8,128)(2,1)} %copy-done.3, bf16[96,2048]{1,0:T(8,128)(2,1)} %copy-done.6, bf16[96,2048]{1,0:T(8,128)(2,1)} %copy-done.10, bf16[1,512,4096]{2,1,0:T(8,128)(2,1)} %refs_11_.1, bf16[1,512,4096]{2,1,0:T(8,128)(2,1)} %refs_12_.1, ...), custom_call_target="tpu_custom_call" | custom-call | flops 3221225472 | bytes 18350080 | tf_op jit(solution)/shard_map/hidden/pallas_call | solution.py:266
  229.5 17.7 %hidden.3.refs_1_ = bf16[576,1024]{1,0:T(8,128)(2,1)} custom-call(bf16[192,2048]{1,0:T(8,128)(2,1)} %collective-permute-done.4.refs_0_, bf16[192,2048]{1,0:T(8,128)(2,1)} %collective-permute-done.5.refs_1_, bf16[96,2048]{1,0:T(8,128)(2,1)} %copy-done.16, bf16[96,2048]{1,0:T(8,128)(2,1)} %copy-done.17, bf16[96,2048]{1,0:T(8,128)(2,1)} %copy-done.7, ...), custom_call_target="tpu_custom_call" | custom-call | flops 9663676416 | bytes 21495808 | tf_op jit(solution)/shard_map/hidden/pallas_call | solution.py:266
  248.5 5.5 %down.3 = (bf16[96,2048]{1,0:T(8,128)(2,1)S(1)}, bf16[96,2048]{1,0:T(8,128)(2,1)S(1)}, bf16[96,2048]{1,0:T(8,128)(2,1)S(1)}, bf16[96,2048]{1,0:T(8,128)(2,1)S(1)...) custom-call(bf16[192,1024]{1,0:T(8,128)(2,1)S(1)} %hidden.2.refs_0_, ...), custom_call_target="tpu_custom_call" | custom-call | flops 3221225472 | bytes 8912896 | tf_op jit(solution)/shard_map/down/pallas_call | solution.py:306
  259.2 5.3 %down.2 = (bf16[192,2048]{1,0:T(8,128)(2,1)S(1)}, bf16[192,2048]{1,0:T(8,128)(2,1)S(1)}, bf16[192,2048]{1,0:T(8,128)(2,1)S(1)}, bf16[96,2048]{1,0:T(8,128)(2,1)S(1)}, bf16[96,2048]{1,0:T(8,128)(2,1)S(1)}) custom-call(bf16[192,1024]{1,0:T(8,128)(2,1)S(1)} %hidden.2.refs_0_, bf16[576,1024]{1,0:T(8,128)(2,1)S(1)} %copy-done.2, ...), custom_call_target="tpu_custom_call" | custom-call | flops 3221225472 | bytes 8912896 | tf_op jit(solution)/shard_map/down/pallas_call | solution.py:306
  268.2 18.7 %collective-permute-done.17 = bf16[96,2048]{1,0:T(8,128)(2,1)S(1)} collective-permute-done((bf16[96,2048]{1,0:T(8,128)(2,1)S(1)}, bf16[96,2048]{1,0:T(8,128)(2,1)S(1)}, u32[]{:S(2)}, u32[]{:S(2)}) %collective-permute-start.17) | collective-permute-done | bytes 393248 | tf_op jit(solution)/shard_map/ppermute | solution.py:25
  291.0 4.8 %collective-permute-done.25 = bf16[96,1024]{1,0:T(8,128)(2,1)S(1)} collective-permute-done((bf16[96,1024]{1,0:T(8,128)(2,1)S(1)}, bf16[96,1024]{1,0:T(8,128)(2,1)S(1)}, u32[]{:S(2)}, u32[]{:S(2)}) %collective-permute-start.25) | collective-permute-done | bytes 196640 | tf_op jit(solution)/shard_map/ppermute | solution.py:25
  297.7 11.1 %collective-permute-done.18 = bf16[192,2048]{1,0:T(8,128)(2,1)S(1)} collective-permute-done((bf16[192,2048]{1,0:T(8,128)(2,1)S(1)}, bf16[192,2048]{1,0:T(8,128)(2,1)S(1)}, u32[]{:S(2)}, u32[]{:S(2)}) %collective-permute-start.18) | collective-permute-done | bytes 786464 | tf_op jit(solution)/shard_map/ppermute | solution.py:25
  308.8 4.8 %collective-permute-done.16 = bf16[192,2048]{1,0:T(8,128)(2,1)S(1)} collective-permute-done((bf16[192,2048]{1,0:T(8,128)(2,1)S(1)}, bf16[192,2048]{1,0:T(8,128)(2,1)S(1)}, u32[]{:S(2)}, u32[]{:S(2)}) %collective-permute-start.16) | collective-permute-done | bytes 786464 | tf_op jit(solution)/shard_map/ppermute | solution.py:25
  319.3 4.1 %collective-permute-done.24 = bf16[96,2048]{1,0:T(8,128)(2,1)S(1)} collective-permute-done((bf16[96,2048]{1,0:T(8,128)(2,1)S(1)}, bf16[96,2048]{1,0:T(8,128)(2,1)S(1)}, u32[]{:S(2)}, u32[]{:S(2)}) %collective-permute-start.24) | collective-permute-done | bytes 393248 | tf_op jit(solution)/shard_map/ppermute | solution.py:25
  331.3 4.4 %all-to-all-start.3 = ((bf16[8,12,4096]{2,1,0:T(8,128)(2,1)}), bf16[8,12,4096]{2,1,0:T(8,128)(2,1)S(1)}, u32[]{:S(2)}, u32[]{:S(2)}) async-start(bf16[8,12,4096]{2,1,0:T(8,128)(2,1)} %pad_maximum_fusion), calls=%async_computation.3 | async-start | bytes 2097152 | tf_op jit(solution)/shard_map/all_to_all | solution.py:474
  340.5 5.8 %all-to-all-done.3 = bf16[8,12,4096]{2,1,0:T(8,128)(2,1)S(1)} async-done(((bf16[8,12,4096]{2,1,0:T(8,128)(2,1)}), bf16[8,12,4096]{2,1,0:T(8,128)(2,1)S(1)}, u32[]{:S(2)}, u32[]{:S(2)}) %all-to-all-start.3) | async-done | bytes 786464 | tf_op jit(solution)/shard_map/all_to_all | solution.py:474
  (162 shorter events, 79.5 us)
Async XLA Ops:
  7.6 59.9 %all-to-all-start = ((bf16[16,2,512,128]{3,2,1,0:T(8,128)(2,1)}), bf16[16,2,512,128]{3,2,1,0:T(8,128)(2,1)}, u32[]{:S(2)}, u32[]{:S(2)}) async-start(bf16[16,2,512,128]{3,2,1,0:T(8,128)(2,1)} %select.148), calls=%async_computation | async-start | bytes 8388608 | tf_op jit(solution)/shard_map/all_to_all | solution.py:357
  89.9 30.3 %all-to-all-start.1 = ((bf16[8,32,4096]{2,1,0:T(8,128)(2,1)}), bf16[8,32,4096]{2,1,0:T(8,128)(2,1)S(1)}, u32[]{:S(2)}, u32[]{:S(2)}) async-start(bf16[8,32,4096]{2,1,0:T(8,128)(2,1)} %bitcast.36), calls=%async_computation.1 | async-start | bytes 4194304 | tf_op jit(solution)/shard_map/all_to_all | solution.py:377
  95.4 115.0 %collective-permute-start.2 = (bf16[1,512,4096]{2,1,0:T(8,128)(2,1)}, bf16[1,512,4096]{2,1,0:T(8,128)(2,1)}, u32[]{:S(2)}, u32[]{:S(2)}) collective-permute-start(bf16[1,512,4096]{2,1,0:T(8,128)(2,1)} %refs_11_.1), channel_id=1, source_target_pairs={{0,8},{8,0},{1,9},{9,1},{2,10},{10,2},{3,11},{11,3},{4,12},{12,4},... | collective-permute-start | bytes 12582920 | tf_op jit(solution)/shard_map/ppermute | solution.py:29
  95.5 119.1 %collective-permute-start.3 = (bf16[1,512,4096]{2,1,0:T(8,128)(2,1)}, bf16[1,512,4096]{2,1,0:T(8,128)(2,1)}, u32[]{:S(2)}, u32[]{:S(2)}) collective-permute-start(bf16[1,512,4096]{2,1,0:T(8,128)(2,1)} %refs_12_.1), channel_id=1, source_target_pairs={{0,8},{8,0},{1,9},{9,1},{2,10},{10,2},{3,11},{11,3},{4,12},{12,4},... | collective-permute-start | bytes 12582920 | tf_op jit(solution)/shard_map/ppermute | solution.py:29
  122.3 18.6 %all-to-all-start.2 = ((bf16[8,12,4096]{2,1,0:T(8,128)(2,1)}), bf16[8,12,4096]{2,1,0:T(8,128)(2,1)S(1)}, u32[]{:S(2)}, u32[]{:S(2)}) async-start(bf16[8,12,4096]{2,1,0:T(8,128)(2,1)} %all_to_all.22), calls=%async_computation.2 | async-start | bytes 2097152 | tf_op jit(solution)/shard_map/all_to_all | solution.py:401
  125.9 121.3 %collective-permute-start.14 = (bf16[1,512,4096]{2,1,0:T(8,128)(2,1)}, bf16[1,512,4096]{2,1,0:T(8,128)(2,1)}, u32[]{:S(2)}, u32[]{:S(2)}) collective-permute-start(bf16[1,512,4096]{2,1,0:T(8,128)(2,1)} %refs_2_.3), channel_id=1, source_target_pairs={{0,8},{8,0},{1,9},{9,1},{2,10},{10,2},{3,11},{11,3},{4,12},{12,4},... | collective-permute-start | bytes 12582920 | tf_op jit(solution)/shard_map/ppermute | solution.py:29
  163.1 18.8 %collective-permute-start.4 = (bf16[192,2048]{1,0:T(8,128)(2,1)S(1)}, bf16[192,2048]{1,0:T(8,128)(2,1)}, u32[]{:S(2)}, u32[]{:S(2)}) collective-permute-start(bf16[192,2048]{1,0:T(8,128)(2,1)S(1)} %pad_maximum_fusion.1.refs_0_), channel_id=1, source_target_pairs={{0,32},{32,64},{64,96},{96,0},{1,33},{33,65},{65,97},{97,1},{2,34}... | collective-permute-start | bytes 2359304 | tf_op jit(solution)/shard_map/ppermute | solution.py:25
  169.6 17.2 %collective-permute-start.5 = (bf16[192,2048]{1,0:T(8,128)(2,1)S(1)}, bf16[192,2048]{1,0:T(8,128)(2,1)}, u32[]{:S(2)}, u32[]{:S(2)}) collective-permute-start(bf16[192,2048]{1,0:T(8,128)(2,1)S(1)} %pad_maximum_fusion.1.refs_0_), channel_id=1, source_target_pairs={{0,96},{32,0},{64,32},{96,64},{1,97},{33,1},{65,33},{97,65},{2,98}... | collective-permute-start | bytes 2359304 | tf_op jit(solution)/shard_map/ppermute | solution.py:25
  181.9 28.5 %collective-permute-start.10 = (bf16[192,2048]{1,0:T(8,128)(2,1)S(1)}, bf16[192,2048]{1,0:T(8,128)(2,1)S(1)}, u32[]{:S(2)}, u32[]{:S(2)}) collective-permute-start(bf16[192,2048]{1,0:T(8,128)(2,1)S(1)} %pad_maximum_fusion.2), channel_id=1, source_target_pairs={{0,16},{16,0},{1,17},{17,1},{2,18},{18,2},{3,19},{19,3},{4,20},{20... | collective-permute-start | bytes 2359304 | tf_op jit(solution)/shard_map/ppermute | solution.py:29
  186.8 21.5 %collective-permute-start.1 = (bf16[96,2048]{1,0:T(8,128)(2,1)S(1)}, bf16[96,2048]{1,0:T(8,128)(2,1)S(1)}, u32[]{:S(2)}, u32[]{:S(2)}) collective-permute-start(bf16[96,2048]{1,0:T(8,128)(2,1)S(1)} %get-tuple-element.55.refs_1_), channel_id=1, source_target_pairs={{0,16},{16,0},{1,17},{17,1},{2,18},{18,2},{3,19},{19,3},{4,20},{20... | collective-permute-start | bytes 1179656 | tf_op jit(solution)/shard_map/ppermute | solution.py:29
  208.4 20.0 %collective-permute-start.13 = (bf16[96,2048]{1,0:T(8,128)(2,1)S(1)}, bf16[96,2048]{1,0:T(8,128)(2,1)S(1)}, u32[]{:S(2)}, u32[]{:S(2)}) collective-permute-start(bf16[96,2048]{1,0:T(8,128)(2,1)S(1)} %pad_maximum_fusion.6), channel_id=1, source_target_pairs={{0,16},{16,0},{1,17},{17,1},{2,18},{18,2},{3,19},{19,3},{4,20},{20... | collective-permute-start | bytes 1179656 | tf_op jit(solution)/shard_map/ppermute | solution.py:29
  210.4 18.1 %collective-permute-start.6 = (bf16[96,2048]{1,0:T(8,128)(2,1)S(1)}, bf16[96,2048]{1,0:T(8,128)(2,1)S(1)}, u32[]{:S(2)}, u32[]{:S(2)}) collective-permute-start(bf16[96,2048]{1,0:T(8,128)(2,1)S(1)} %slice.98), channel_id=1, source_target_pairs={{0,32},{32,64},{64,96},{96,0},{1,33},{33,65},{65,97},{97,1},{2,34}... | collective-permute-start | bytes 1179656 | tf_op jit(solution)/shard_map/ppermute | solution.py:25
  210.4 18.1 %collective-permute-start.7 = (bf16[96,2048]{1,0:T(8,128)(2,1)S(1)}, bf16[96,2048]{1,0:T(8,128)(2,1)S(1)}, u32[]{:S(2)}, u32[]{:S(2)}) collective-permute-start(bf16[96,2048]{1,0:T(8,128)(2,1)S(1)} %slice.99), channel_id=1, source_target_pairs={{0,96},{32,0},{64,32},{96,64},{1,97},{33,1},{65,33},{97,65},{2,98}... | collective-permute-start | bytes 1179656 | tf_op jit(solution)/shard_map/ppermute | solution.py:25
  214.6 41.5 %collective-permute-start.28 = (bf16[2,2,256,128]{3,2,1,0:T(8,128)(2,1)S(1)}, bf16[2,2,256,128]{3,2,1,0:T(8,128)(2,1)S(1)}, u32[]{:S(2)}, u32[]{:S(2)}) collective-permute-start(bf16[2,2,256,128]{3,2,1,0:T(8,128)(2,1)S(1)} %pad_maximum_fusion.9), channel_id=1, source_target_pairs={{0,16},{16,0},{1,17},{17,1},{2,18},{18,2},{3,19},{19,3},{4,20},{20... | collective-permute-start | bytes 786440 | tf_op jit(solution)/shard_map/ppermute | solution.py:29
  256.2 80.4 %collective-permute-start.29 = (bf16[4,2,256,128]{3,2,1,0:T(8,128)(2,1)S(1)}, bf16[4,2,256,128]{3,2,1,0:T(8,128)(2,1)}, u32[]{:S(2)}, u32[]{:S(2)}) collective-permute-start(bf16[4,2,256,128]{3,2,1,0:T(8,128)(2,1)S(1)} %pad_maximum_fusion.5.refs_0_), channel_id=1, source_target_pairs={{0,32},{32,64},{64,96},{96,0},{1,33},{33,65},{65,97},{97,1},{2,34}... | collective-permute-start | bytes 1572872 | tf_op jit(solution)/shard_map/ppermute | solution.py:25
  256.3 80.3 %collective-permute-start.30 = (bf16[4,2,256,128]{3,2,1,0:T(8,128)(2,1)S(1)}, bf16[4,2,256,128]{3,2,1,0:T(8,128)(2,1)}, u32[]{:S(2)}, u32[]{:S(2)}) collective-permute-start(bf16[4,2,256,128]{3,2,1,0:T(8,128)(2,1)S(1)} %pad_maximum_fusion.5.refs_0_), channel_id=1, source_target_pairs={{0,64},{32,96},{64,0},{96,32},{1,65},{33,97},{65,1},{97,33},{2,66}... | collective-permute-start | bytes 1572872 | tf_op jit(solution)/shard_map/ppermute | solution.py:25
  257.7 33.0 %collective-permute-start.21 = (bf16[192,2048]{1,0:T(8,128)(2,1)S(1)}, bf16[192,2048]{1,0:T(8,128)(2,1)S(1)}, u32[]{:S(2)}, u32[]{:S(2)}) collective-permute-start(bf16[192,2048]{1,0:T(8,128)(2,1)S(1)} %get-tuple-element.33), channel_id=1, source_target_pairs={{0,16},{16,0},{1,17},{17,1},{2,18},{18,2},{3,19},{19,3},{4,20},{20... | collective-permute-start | bytes 2359304 | tf_op jit(solution)/shard_map/ppermute | solution.py:29
  264.6 22.2 %collective-permute-start.17 = (bf16[96,2048]{1,0:T(8,128)(2,1)S(1)}, bf16[96,2048]{1,0:T(8,128)(2,1)S(1)}, u32[]{:S(2)}, u32[]{:S(2)}) collective-permute-start(bf16[96,2048]{1,0:T(8,128)(2,1)S(1)} %get-tuple-element.29), channel_id=1, source_target_pairs={{0,32},{32,64},{64,96},{96,0},{1,33},{33,65},{65,97},{97,1},{2,34}... | collective-permute-start | bytes 1179656 | tf_op jit(solution)/shard_map/ppermute | solution.py:25
  267.6 19.4 %collective-permute-start.15 = (bf16[96,2048]{1,0:T(8,128)(2,1)S(1)}, bf16[96,2048]{1,0:T(8,128)(2,1)S(1)}, u32[]{:S(2)}, u32[]{:S(2)}) collective-permute-start(bf16[96,2048]{1,0:T(8,128)(2,1)S(1)} %get-tuple-element.27), channel_id=1, source_target_pairs={{0,96},{32,0},{64,32},{96,64},{1,97},{33,1},{65,33},{97,65},{2,98}... | collective-permute-start | bytes 1179656 | tf_op jit(solution)/shard_map/ppermute | solution.py:25
  290.7 18.0 %collective-permute-start.18 = (bf16[192,2048]{1,0:T(8,128)(2,1)S(1)}, bf16[192,2048]{1,0:T(8,128)(2,1)S(1)}, u32[]{:S(2)}, u32[]{:S(2)}) collective-permute-start(bf16[192,2048]{1,0:T(8,128)(2,1)S(1)} %pad_maximum_fusion.4), channel_id=1, source_target_pairs={{0,32},{32,64},{64,96},{96,0},{1,33},{33,65},{65,97},{97,1},{2,34}... | collective-permute-start | bytes 2359304 | tf_op jit(solution)/shard_map/ppermute | solution.py:25
  295.8 17.7 %collective-permute-start.16 = (bf16[192,2048]{1,0:T(8,128)(2,1)S(1)}, bf16[192,2048]{1,0:T(8,128)(2,1)S(1)}, u32[]{:S(2)}, u32[]{:S(2)}) collective-permute-start(bf16[192,2048]{1,0:T(8,128)(2,1)S(1)} %pad_maximum_fusion.3), channel_id=1, source_target_pairs={{0,96},{32,0},{64,32},{96,64},{1,97},{33,1},{65,33},{97,65},{2,98}... | collective-permute-start | bytes 2359304 | tf_op jit(solution)/shard_map/ppermute | solution.py:25
  296.0 18.7 %collective-permute-start.20 = (bf16[96,2048]{1,0:T(8,128)(2,1)S(1)}, bf16[96,2048]{1,0:T(8,128)(2,1)S(1)}, u32[]{:S(2)}, u32[]{:S(2)}) collective-permute-start(bf16[96,2048]{1,0:T(8,128)(2,1)S(1)} %get-tuple-element.31), channel_id=1, source_target_pairs={{0,16},{16,0},{1,17},{17,1},{2,18},{18,2},{3,19},{19,3},{4,20},{20... | collective-permute-start | bytes 1179656 | tf_op jit(solution)/shard_map/ppermute | solution.py:29
  314.7 21.8 %collective-permute-start.31 = (bf16[4,2,256,128]{3,2,1,0:T(8,128)(2,1)S(1)}, bf16[4,2,256,128]{3,2,1,0:T(8,128)(2,1)}, u32[]{:S(2)}, u32[]{:S(2)}) collective-permute-start(bf16[4,2,256,128]{3,2,1,0:T(8,128)(2,1)S(1)} %pad_maximum_fusion.5.refs_0_), channel_id=1, source_target_pairs={{0,96},{32,0},{64,32},{96,64},{1,97},{33,1},{65,33},{97,65},{2,98}... | collective-permute-start | bytes 1572872 | tf_op jit(solution)/shard_map/ppermute | solution.py:25
  331.3 15.0 %all-to-all-start.3 = ((bf16[8,12,4096]{2,1,0:T(8,128)(2,1)}), bf16[8,12,4096]{2,1,0:T(8,128)(2,1)S(1)}, u32[]{:S(2)}, u32[]{:S(2)}) async-start(bf16[8,12,4096]{2,1,0:T(8,128)(2,1)} %pad_maximum_fusion), calls=%async_computation.3 | async-start | bytes 2097152 | tf_op jit(solution)/shard_map/all_to_all | solution.py:474
  (31 other events, 484.1 us)
where the time goes:
time: 349 us; the launch traced here: 348 us
  waiting for transfers between devices  194 us (56%)
  Pallas kernels  65.2 us (19%)
  starting transfers between devices  56.8 us (16%)
  local copies, waits for them, and re-layouts  14.3 us (4%)
  other arithmetic  9.97 us (3%)
  matrix products  6.48 us (2%)
    ppermute x19, waiting for transfers between devices, shift_z(): return lax.ppermute(x, 'z', [(i, (i + by) % n) for i in range(n)])  76.2 us
    all_to_all x1, waiting for transfers between devices, local(): lax.all_to_all(outgoing, GROUP, split_axis=0, concat_axis=0, tiled=True)  49.2 us
    pallas_call x2, Pallas kernels, hidden_units(): pl.pallas_call(functools.partial(hidden_body, moves), grid=(2 * half,), i...  30 us
    all_to_all x1, waiting for transfers between devices, local(): lax.all_to_all(partial, TENSOR, split_axis=0, concat_axis=0, tiled=True)  24.2 us
    ppermute x13, waiting for transfers between devices, swap(): return lax.ppermute(x, axis, [(0, 1), (1, 0)])  23.3 us
    ppermute x19, starting transfers between devices, shift_z(): return lax.ppermute(x, 'z', [(i, (i + by) % n) for i in range(n)])  19.4 us
    pallas_call x1, Pallas kernels, attention(): pl.pallas_call(functools.partial(attend_body, begin, end, per), grid_spec...  17.5 us
    ppermute x13, starting transfers between devices, swap(): return lax.ppermute(x, axis, [(0, 1), (1, 0)])  16.7 us
  transfers between devices with their start and end apart: 36, of which 20 were waited for; matrix products, arithmetic and copies ran while one was open for 5% of the time, Pallas kernels for 13%

commit v1 on v0

--- a/solution.py
+++ b/solution.py
@@ -16,7 +16,6 @@
 CAP = 12
 GROUP = ("z", "xh", "c")
 TENSOR = ("xl", "y")
-SPLIT = 2048
 PER = 4
 
 
@@ -31,6 +30,15 @@
 
 def plus(*terms):
     return sum(t.astype(jnp.float32) for t in terms)
+
+
+def halved(routes):
+    rows = routes.shape[0]
+    routes = routes.reshape(rows, EXPERTS, CAP)
+    none = jnp.zeros_like(routes)
+    upper = jnp.concatenate([routes, none], axis=2).reshape(rows, -1)
+    lower = jnp.concatenate([none, routes], axis=2).reshape(rows, -1)
+    return jnp.concatenate([upper, lower])
 
 
 def select_body(picked, scale_ref, codes_ref, *refs):
@@ -38,7 +46,7 @@
     pool = codes_ref.shape[1]
     for b in range(pool):
         for c in range(2):
-            s = scale_ref[c, b, 0]
+            s = scale_ref[c, 0, b]
             pool_sc[b, c] = (codes_ref[c, b].astype(jnp.float32) * s).astype(jnp.bfloat16)
     copies, row = [], 0
     for i, out in enumerate(outs):
@@ -234,9 +242,12 @@
     @pl.when(step == 0)
     def _():
         copies = []
-        for i, (ref, (r, c)) in enumerate(zip(ins, moves)):
-            dst = x_sc.at[pl.ds(r, ref.shape[0]), pl.ds(c, ref.shape[1])]
-            copies.append(pltpu.make_async_copy(ref, dst, sem.at[i]))
+        for ref, (places, c) in zip(ins, moves):
+            n = ref.shape[0] // len(places)
+            for i, r in enumerate(places):
+                src = ref.at[pl.ds(i * n, n)]
+                dst = x_sc.at[pl.ds(r, n), pl.ds(c, ref.shape[1])]
+                copies.append(pltpu.make_async_copy(src, dst, sem.at[len(copies)]))
         for copy in copies:
             copy.start()
         for copy in copies:
@@ -271,7 +282,7 @@
         out_shape=jax.ShapeDtypeStruct((rows, 2 * units), jnp.bfloat16),
         scratch_shapes=[
             pltpu.VMEM((rows, width), jnp.bfloat16),
-            pltpu.SemaphoreType.DMA((len(ins),)),
+            pltpu.SemaphoreType.DMA((sum(len(m[0]) for m in moves),)),
         ],
         compiler_params=pltpu.CompilerParams(vmem_limit_bytes=56_000_000),
         cost_estimate=pl.CostEstimate(
@@ -352,7 +363,7 @@
     mine = jnp.logical_and(owners == my_group, position < prefix_blocks[:, None])
     picked = jnp.sum(jnp.where(mine, block_table % pool, 0), axis=1)
     (outgoing,) = select_blocks(
-        picked, pool_scales, pool_codes.reshape(2, pool, pblock, dim), (pblock,)
+        picked, jnp.swapaxes(pool_scales, 1, 2), pool_codes.reshape(2, pool, pblock, dim), (pblock,)
     )
     got = lax.all_to_all(outgoing, GROUP, split_axis=0, concat_axis=0, tiled=True)
     my_row = lax.dynamic_index_in_dim(block_table, my_group, 0, keepdims=False)
@@ -392,39 +403,46 @@
     slot = (pair_ids * CAP + rank).reshape(tok_dev, TOP)
     slot_iota = lax.broadcasted_iota(jnp.int32, (EXPERTS * CAP,), 0)
     matches = slot[:, :, None] == slot_iota[None, None, :]
-    route_rows = jnp.any(matches, axis=1).astype(jnp.bfloat16)
+    route_rows = halved(jnp.any(matches, axis=1).astype(jnp.bfloat16))
     pair_weight = jnp.stack([expert_share, 1.0 - expert_share], axis=1)
-    combine = jnp.sum(jnp.where(matches, pair_weight[:, :, None], 0.0), axis=1)
-    outbound = jnp.einsum(
-        "ie,id->ed", route_rows, normed, preferred_element_type=jnp.float32
-    ).astype(jnp.bfloat16)
-    landed = lax.all_to_all(outbound, TENSOR, split_axis=0, concat_axis=0, tiled=True)
-
-    n = landed.shape[0]
-    a, b = landed[:, :SPLIT], landed[:, SPLIT:]
-    wide = model_width - SPLIT
-    half = wide // 2
+    combine = halved(jnp.sum(jnp.where(matches, pair_weight[:, :, None], 0.0), axis=1))
+    half_width = model_width // 2
+    both = jnp.concatenate([normed[:, :half_width], normed[:, half_width:]])
+    outbound = jnp.einsum("ie,id->ed", route_rows, both, preferred_element_type=jnp.float32)
+    landed = lax.all_to_all(
+        outbound.astype(jnp.bfloat16).reshape(tensors, 2 * CAP, half_width),
+        TENSOR,
+        split_axis=0,
+        concat_axis=0,
+        tiled=True,
+    )
+    n = tensors * CAP
+    a, b = landed[:, :CAP].reshape(n, half_width), landed[:, CAP:].reshape(n, half_width)
+    half = half_width // 2
     ax = swap(a, "xh")
     b_r = shift_z(b, 1)
     b_l = shift_z(b, -1)
     bx = swap(b, "xh")
-    a2 = jnp.concatenate([a, ax])
-    a_r = shift_z(a2, 1)
-    a_l = shift_z(a2, -1)
+    a_r = shift_z(a, 1)
+    a_l = shift_z(a, -1)
+    ax_r = shift_z(ax, 1)
+    ax_l = shift_z(ax, -1)
     bx_rl = swap(jnp.concatenate([b_r, b_l]), "xh")
     b_f1 = shift_z(b_r[:, :half], 1)
     b_f2 = shift_z(b_l[:, half:], -1)
     bx_f = swap(jnp.concatenate([b_f1, b_f2], axis=1), "xh")
-    a_f1 = shift_z(a_r[:n], 1)
-    a_f2 = shift_z(a_l[n:], -1)
-
-    A, B = SPLIT, wide
-    h_o = hidden_units([(a2, (0, 0)), (b, (0, A)), (bx, (n, A))], own, other, 2 * n)
+    a_f1 = shift_z(a_r, 1)
+    a_f2 = shift_z(ax_l, -1)
+
+    w = half_width
+    h_o = hidden_units(
+        [(a, ((0,), 0)), (ax, ((n,), 0)), (b, ((0,), w)), (bx, ((n,), w))], own, other, 2 * n
+    )
     h_r = hidden_units(
-        [(a_r, (0, 0)), (a_l, (2 * n, 0)), (a_f1, (4 * n, 0)), (a_f2, (5 * n, 0))]
-        + [(b_r, (0, A)), (b_l, (2 * n, A))]
-        + [(bx_rl[:n], (n, A)), (bx_rl[n:], (3 * n, A))]
-        + [(b_f1, (4 * n, A)), (b_f2, (4 * n, A + half)), (bx_f, (5 * n, A))],
+        [(a_r, ((0,), 0)), (ax_r, ((n,), 0)), (a_l, ((2 * n,), 0)), (ax_l, ((3 * n,), 0))]
+        + [(a_f1, ((4 * n,), 0)), (a_f2, ((5 * n,), 0)), (b_r, ((0,), w)), (b_l, ((2 * n,), w))]
+        + [(bx_rl, ((n, 3 * n), w)), (b_f1, ((4 * n,), w)), (b_f2, ((4 * n,), w + half))]
+        + [(bx_f, ((5 * n,), w))],
         own,
         other,
         6 * n,
@@ -433,19 +451,19 @@
         [h_o, h_r],
         own,
         other,
-        A,
-        B,
+        w,
+        w,
         [(n, ((0, 0),)), (n, ((1, 0),)), (n, ((1, 2 * n),)), (n, ((1, 4 * n),))]
         + [(n, ((0, n),)), (2 * n, ((1, n), (1, 3 * n))), (n, ((1, 5 * n),))],
     )
-    o_a, r_a, l_a, f1_a, f2_a = down_sums(
+    o_a, r_a, rx_a, l_a, lx_a, f1_a, f2_a = down_sums(
         [h_o, h_r],
         own,
         other,
         0,
-        A,
-        [(2 * n, ((0, 0),)), (2 * n, ((1, 0),)), (2 * n, ((1, 2 * n),))]
-        + [(n, ((1, 4 * n),)), (n, ((1, 5 * n),))],
+        w,
+        [(2 * n, ((0, 0),)), (n, ((1, 0),)), (n, ((1, n),)), (n, ((1, 2 * n),))]
+        + [(n, ((1, 3 * n),)), (n, ((1, 4 * n),)), (n, ((1, 5 * n),))],
     )
 
     bf = jnp.bfloat16
@@ -454,8 +472,8 @@
     u_f = swap(x_f, "xh")
     back1 = shift_z(f1_a, -1)
     back2 = shift_z(f2_a, 1)
-    r_a = jnp.concatenate([plus(r_a[:n], back1), plus(r_a[n:])]).astype(bf)
-    l_a = jnp.concatenate([plus(l_a[:n]), plus(l_a[n:], back2)]).astype(bf)
+    r_a = jnp.concatenate([plus(r_a, back1).astype(bf), rx_a])
+    l_a = jnp.concatenate([l_a, plus(lx_a, back2).astype(bf)])
     t_r = shift_z(r_a, -1)
     t_l = shift_z(l_a, 1)
     s_a = plus(o_a, t_r, t_l)
@@ -469,15 +487,18 @@
     l_b = jnp.concatenate([l_b[:, :half], plus(l_b[:, half:], v2)], axis=1).astype(bf)
     v_r = shift_z(r_b, -1)
     v_l = shift_z(l_b, 1)
-    part_b = plus(o_b, u_o, v_r, v_l)
-    summed = jnp.concatenate([part_a, part_b], axis=1).astype(bf)
-    returned = lax.all_to_all(summed, TENSOR, split_axis=0, concat_axis=0, tiled=True)
+    part_b = plus(o_b, u_o, v_r, v_l).astype(bf)
+    summed = jnp.stack([p.reshape(tensors, CAP, w) for p in (part_a.astype(bf), part_b)], axis=1)
+    returned = lax.all_to_all(
+        summed.reshape(tensors, 2 * CAP, w), TENSOR, split_axis=0, concat_axis=0, tiled=True
+    )
     mixture = jnp.dot(
         combine,
-        returned.astype(jnp.float32),
+        returned.reshape(2 * n, w).astype(jnp.float32),
         precision=lax.Precision.HIGHEST,
         preferred_element_type=jnp.float32,
     )
+    mixture = jnp.concatenate([mixture[:tok_dev], mixture[tok_dev:]], axis=1)
     layer_out = (resid + mixture).astype(jnp.bfloat16)
 
     wanted = my_group * seqs + lax.broadcasted_iota(jnp.int32, (seqs, 1), 0)

time: 349 us -> 336 us (0.963)
  waiting for transfers between devices: 194 us -> 176 us
  starting transfers between devices: 56.8 us -> 62.4 us
    ppermute x19 -> x21, waiting for transfers between devices: 76.2 us -> 68 us  [shift_z(): return lax.ppermute(x, 'z', [(i, (i + by) % n) for i in range(n)])]
    ppermute x19 -> x21, starting transfers between devices: 19.4 us -> 24.5 us  [shift_z(): return lax.ppermute(x, 'z', [(i, (i + by) % n) for i in range(n)])]
    all_to_all x2, waiting for transfers between devices: 20.7 us -> 16 us  [the longest x1 11.6 us: local(): lax.all_to_all(outbound.astype(jnp.bfloat16).reshape(tensors, 2 * CAP, ha...]
    ppermute x13, waiting for transfers between devices: 23.3 us -> 18.8 us  [swap(): return lax.ppermute(x, axis, [(0, 1), (1, 0)])]
    convert_element_type x0 -> x7, other arithmetic: none -> 3.89 us  [the longest x1 1.81 us: local(): part_a.astype(bf)]
  transfers between devices with their start and end apart: 36 -> 38, of which waited for: 20 -> 21; matrix products, arithmetic and copies ran while one was open for 5% -> 6% of each run, Pallas kernels for 13% -> 13%
where the time goes in v1:
time: 336 us; the launch traced here: 334 us
  waiting for transfers between devices  176 us (52%)
  Pallas kernels  65.1 us (19%)
  starting transfers between devices  62.4 us (19%)
  local copies, waits for them, and re-layouts  12.3 us (4%)
  other arithmetic  10.7 us (3%)
  matrix products  6.65 us (2%)
    ppermute x21, waiting for transfers between devices, shift_z(): return lax.ppermute(x, 'z', [(i, (i + by) % n) for i in range(n)])  68 us
    all_to_all x1, waiting for transfers between devices, local(): lax.all_to_all(outgoing, GROUP, split_axis=0, concat_axis=0, tiled=True)  49.2 us
    pallas_call x2, Pallas kernels, hidden_units(): pl.pallas_call(functools.partial(hidden_body, moves), grid=(2 * half,), i...  29.9 us
    ppermute x21, starting transfers between devices, shift_z(): return lax.ppermute(x, 'z', [(i, (i + by) % n) for i in range(n)])  24.5 us
    all_to_all x1, waiting for transfers between devices, local(): lax.all_to_all(partial, TENSOR, split_axis=0, concat_axis=0, tiled=True)  23.9 us
    ppermute x13, waiting for transfers between devices, swap(): return lax.ppermute(x, axis, [(0, 1), (1, 0)])  18.8 us
    pallas_call x1, Pallas kernels, attention(): pl.pallas_call(functools.partial(attend_body, begin, end, per), grid_spec...  17.5 us
    ppermute x13, starting transfers between devices, swap(): return lax.ppermute(x, axis, [(0, 1), (1, 0)])  16.9 us
  transfers between devices with their start and end apart: 38, of which 21 were waited for; matrix products, arithmetic and copies ran while one was open for 6% of the time, Pallas kernels for 13%

profile of v1, /device:TPU:0, one launch (start us, length us, event | category | flops | bytes accessed | tf_op | source)
XLA Modules:
  0.0 334.5 jit_solution(363438687631553238)
XLA Ops:
  2.0 4.2 %select.152 = bf16[16,2,512,128]{3,2,1,0:T(8,128)(2,1)} custom-call(s32[16]{0:T(128)} %fusion.18.picked, f32[2,1,4]{2,1,0:T(1,128)} %bitcast.60, bf16[2,4,512,128]{3,2,1,0:T(8,128)(2,1)} %bitcast.51), custom_call_target="tpu_custom_call" | custom-call | flops 1048576 | bytes 6291456 | tf_op jit(solution)/shard_map/select/pallas_call | solution.py:67
  6.3 8.1 %all-to-all-start = ((bf16[16,2,512,128]{3,2,1,0:T(8,128)(2,1)}), bf16[16,2,512,128]{3,2,1,0:T(8,128)(2,1)}, u32[]{:S(2)}, u32[]{:S(2)}) async-start(bf16[16,2,512,128]{3,2,1,0:T(8,128)(2,1)} %select.152), calls=%async_computation | async-start | bytes 8388608 | tf_op jit(solution)/shard_map/all_to_all | solution.py:368
  16.9 49.2 %all-to-all-done.kv_ref = bf16[16,2,512,128]{3,2,1,0:T(8,128)(2,1)} async-done(((bf16[16,2,512,128]{3,2,1,0:T(8,128)(2,1)}), bf16[16,2,512,128]{3,2,1,0:T(8,128)(2,1)}, u32[]{:S(2)}, u32[]{:S(2)}) %all-to-all-start) | async-done | bytes 4194336 | tf_op jit(solution)/shard_map/all_to_all | solution.py:368
  66.1 17.5 %attend.1 = bf16[256,512]{1,0:T(8,128)(2,1)} custom-call(s32[16]{0:T(128)} %convert_element_type.115.live, bf16[256,512]{1,0:T(8,128)(2,1)} %q_ref.1, bf16[2,256,128]{2,1,0:T(8,128)(2,1)} %new_ref.1, bf16[16,2,512,128]{3,2,1,0:T(8,128)(2,1)} %all-to-all-done.kv_ref), custom_call_target="tpu_custom_call" | custom-call | flops 6442450944 | bytes 5242880 | tf_op jit(solution)/shard_map/attend/pallas_call | solution.py:170
  83.6 4.9 %convolution_convert_fusion = bf16[256,4096]{1,0:T(8,128)(2,1)} fusion(bf16[256,512]{1,0:T(8,128)(2,1)} %attend.1, bf16[512,4096]{1,0:T(8,128)(2,1)} %param.22), kind=kOutput, calls=%fused_computation | convolution fusion | flops 1074790400 | bytes 6553600 | tf_op jit(solution)/shard_map/dot_general | solution.py:386
  88.5 4.6 %all-to-all-start.1 = ((bf16[8,32,4096]{2,1,0:T(8,128)(2,1)}), bf16[8,32,4096]{2,1,0:T(8,128)(2,1)S(1)}, u32[]{:S(2)}, u32[]{:S(2)}) async-start(bf16[8,32,4096]{2,1,0:T(8,128)(2,1)} %bitcast.50), calls=%async_computation.1 | async-start | bytes 4194304 | tf_op jit(solution)/shard_map/all_to_all | solution.py:388
  94.9 23.9 %all-to-all-done.1 = bf16[8,32,4096]{2,1,0:T(8,128)(2,1)S(1)} async-done(((bf16[8,32,4096]{2,1,0:T(8,128)(2,1)}), bf16[8,32,4096]{2,1,0:T(8,128)(2,1)S(1)}, u32[]{:S(2)}, u32[]{:S(2)}) %all-to-all-start.1) | async-done | bytes 2097184 | tf_op jit(solution)/shard_map/all_to_all | solution.py:388
  120.8 3.6 %all-to-all-start.2 = ((bf16[8,24,2048]{2,1,0:T(8,128)(2,1)}), bf16[8,24,2048]{2,1,0:T(8,128)(2,1)S(1)}, u32[]{:S(2)}, u32[]{:S(2)}) async-start(bf16[8,24,2048]{2,1,0:T(8,128)(2,1)} %bitcast.12), calls=%async_computation.2 | async-start | bytes 1572864 | tf_op jit(solution)/shard_map/all_to_all | solution.py:412
  125.0 11.6 %all-to-all-done.2 = bf16[8,24,2048]{2,1,0:T(8,128)(2,1)S(1)} async-done(((bf16[8,24,2048]{2,1,0:T(8,128)(2,1)}), bf16[8,24,2048]{2,1,0:T(8,128)(2,1)S(1)}, u32[]{:S(2)}, u32[]{:S(2)}) %all-to-all-start.2) | async-done | bytes 786464 | tf_op jit(solution)/shard_map/all_to_all | solution.py:412
  140.6 9.9 %collective-permute-done.refs_1_ = bf16[96,2048]{1,0:T(8,128)(2,1)} collective-permute-done((bf16[96,2048]{1,0:T(8,128)(2,1)S(1)}, bf16[96,2048]{1,0:T(8,128)(2,1)}, u32[]{:S(2)}, u32[]{:S(2)}) %collective-permute-start) | collective-permute-done | bytes 393248 | tf_op jit(solution)/shard_map/ppermute | solution.py:28
  150.9 6.4 %collective-permute-done.1.refs_3_ = bf16[96,2048]{1,0:T(8,128)(2,1)} collective-permute-done((bf16[96,2048]{1,0:T(8,128)(2,1)S(1)}, bf16[96,2048]{1,0:T(8,128)(2,1)}, u32[]{:S(2)}, u32[]{:S(2)}) %collective-permute-start.1) | collective-permute-done | bytes 393248 | tf_op jit(solution)/shard_map/ppermute | solution.py:28
  160.5 7.4 %collective-permute-done.10.refs_6_ = bf16[96,2048]{1,0:T(8,128)(2,1)S(1)} collective-permute-done((bf16[96,2048]{1,0:T(8,128)(2,1)S(1)}, bf16[96,2048]{1,0:T(8,128)(2,1)S(1)}, u32[]{:S(2)}, u32[]{:S(2)}) %collective-permute-start.10) | collective-permute-done | bytes 393248 | tf_op jit(solution)/shard_map/ppermute | solution.py:24
  170.1 6.5 %collective-permute-done.11.refs_7_ = bf16[96,2048]{1,0:T(8,128)(2,1)S(1)} collective-permute-done((bf16[96,2048]{1,0:T(8,128)(2,1)S(1)}, bf16[96,2048]{1,0:T(8,128)(2,1)S(1)}, u32[]{:S(2)}, u32[]{:S(2)}) %collective-permute-start.11) | collective-permute-done | bytes 393248 | tf_op jit(solution)/shard_map/ppermute | solution.py:24
  190.6 5.8 %collective-permute-done.7.refs_3_ = bf16[96,2048]{1,0:T(8,128)(2,1)} collective-permute-done((bf16[96,2048]{1,0:T(8,128)(2,1)}, bf16[96,2048]{1,0:T(8,128)(2,1)}, u32[]{:S(2)}, u32[]{:S(2)}) %collective-permute-start.7) | collective-permute-done | bytes 393248 | tf_op jit(solution)/shard_map/ppermute | solution.py:24
  201.7 12.3 %hidden.2.refs_0_ = bf16[192,1024]{1,0:T(8,128)(2,1)S(1)} custom-call(bf16[96,2048]{1,0:T(8,128)(2,1)} %copy-done.5, bf16[96,2048]{1,0:T(8,128)(2,1)} %collective-permute-done.refs_1_, bf16[96,2048]{1,0:T(8,128)(2,1)} %copy-done.6, bf16[96,2048]{1,0:T(8,128)(2,1)} %collective-permute-done.1.refs_3_, bf16[1,512,4096]{2,1,0:T(8,128)(2,1)} %refs_12_.1, ...), custom_call_target="tpu_custom_call" | custom-call | flops 3221225472 | bytes 18350080 | tf_op jit(solution)/shard_map/hidden/pallas_call | solution.py:277
  216.6 17.6 %hidden.3.refs_1_ = bf16[576,1024]{1,0:T(8,128)(2,1)} custom-call(bf16[96,2048]{1,0:T(8,128)(2,1)} %copy-done.15, bf16[96,2048]{1,0:T(8,128)(2,1)} %copy-done.17, bf16[96,2048]{1,0:T(8,128)(2,1)} %copy-done.16, bf16[96,2048]{1,0:T(8,128)(2,1)} %collective-permute-done.7.refs_3_, bf16[96,2048]{1,0:T(8,128)(2,1)} %copy-done.18, bf16[96,2048]{1,0:T(8,128)(2,1)} %copy-done.20, ...), custom_call_target="tpu_custom_call" | custom-call | flops 9663676416 | bytes 21495808 | tf_op jit(solution)/shard_map/hidden/pallas_call | solution.py:277
  235.6 5.5 %down.3 = (bf16[96,2048]{1,0:T(8,128)(2,1)S(1)}, bf16[96,2048]{1,0:T(8,128)(2,1)S(1)}, bf16[96,2048]{1,0:T(8,128)(2,1)S(1)}, bf16[96,2048]{1,0:T(8,128)(2,1)S(1)...) custom-call(bf16[192,1024]{1,0:T(8,128)(2,1)S(1)} %hidden.2.refs_0_, ...), custom_call_target="tpu_custom_call" | custom-call | flops 3221225472 | bytes 8912896 | tf_op jit(solution)/shard_map/down/pallas_call | solution.py:317
  248.2 5.3 %down.2 = (bf16[192,2048]{1,0:T(8,128)(2,1)S(1)}, bf16[96,2048]{1,0:T(8,128)(2,1)S(1)}, bf16[96,2048]{1,0:T(8,128)(2,1)S(1)}, bf16[96,2048]{1,0:T(8,128)(2,1)S(1...) custom-call(bf16[192,1024]{1,0:T(8,128)(2,1)S(1)} %hidden.2.refs_0_, ...), custom_call_target="tpu_custom_call" | custom-call | flops 3221225472 | bytes 8912896 | tf_op jit(solution)/shard_map/down/pallas_call | solution.py:317
  257.0 16.3 %collective-permute-done.19 = bf16[96,2048]{1,0:T(8,128)(2,1)S(1)} collective-permute-done((bf16[96,2048]{1,0:T(8,128)(2,1)S(1)}, bf16[96,2048]{1,0:T(8,128)(2,1)S(1)}, u32[]{:S(2)}, u32[]{:S(2)}) %collective-permute-start.19) | collective-permute-done | bytes 393248 | tf_op jit(solution)/shard_map/ppermute | solution.py:24
  277.4 5.0 %collective-permute-done.27 = bf16[96,1024]{1,0:T(8,128)(2,1)S(1)} collective-permute-done((bf16[96,1024]{1,0:T(8,128)(2,1)S(1)}, bf16[96,1024]{1,0:T(8,128)(2,1)S(1)}, u32[]{:S(2)}, u32[]{:S(2)}) %collective-permute-start.27) | collective-permute-done | bytes 196640 | tf_op jit(solution)/shard_map/ppermute | solution.py:24
  285.4 10.1 %collective-permute-done.20 = bf16[192,2048]{1,0:T(8,128)(2,1)S(1)} collective-permute-done((bf16[192,2048]{1,0:T(8,128)(2,1)S(1)}, bf16[192,2048]{1,0:T(8,128)(2,1)S(1)}, u32[]{:S(2)}, u32[]{:S(2)}) %collective-permute-start.20) | collective-permute-done | bytes 786464 | tf_op jit(solution)/shard_map/ppermute | solution.py:24
  300.0 4.5 %collective-permute-done.28 = bf16[96,2048]{1,0:T(8,128)(2,1)S(1)} collective-permute-done((bf16[96,2048]{1,0:T(8,128)(2,1)S(1)}, bf16[96,2048]{1,0:T(8,128)(2,1)S(1)}, u32[]{:S(2)}, u32[]{:S(2)}) %collective-permute-start.28) | collective-permute-done | bytes 393248 | tf_op jit(solution)/shard_map/ppermute | solution.py:24
  318.9 4.7 %all-to-all-start.3 = ((bf16[8,24,2048]{2,1,0:T(8,128)(2,1)}), bf16[8,24,2048]{2,1,0:T(8,128)(2,1)S(1)}, u32[]{:S(2)}, u32[]{:S(2)}) async-start(bf16[8,24,2048]{2,1,0:T(8,128)(2,1)} %copy.88), calls=%async_computation.3 | async-start | bytes 1572864 | tf_op jit(solution)/shard_map/all_to_all | solution.py:492
  328.7 4.5 %all-to-all-done.3 = bf16[8,24,2048]{2,1,0:T(8,128)(2,1)S(1)} async-done(((bf16[8,24,2048]{2,1,0:T(8,128)(2,1)}), bf16[8,24,2048]{2,1,0:T(8,128)(2,1)S(1)}, u32[]{:S(2)}, u32[]{:S(2)}) %all-to-all-start.3) | async-done | bytes 786464 | tf_op jit(solution)/shard_map/all_to_all | solution.py:492
  (181 shorter events, 83.7 us)
Async XLA Ops:
  6.3 59.9 %all-to-all-start = ((bf16[16,2,512,128]{3,2,1,0:T(8,128)(2,1)}), bf16[16,2,512,128]{3,2,1,0:T(8,128)(2,1)}, u32[]{:S(2)}, u32[]{:S(2)}) async-start(bf16[16,2,512,128]{3,2,1,0:T(8,128)(2,1)} %select.152), calls=%async_computation | async-start | bytes 8388608 | tf_op jit(solution)/shard_map/all_to_all | solution.py:368
  88.5 30.3 %all-to-all-start.1 = ((bf16[8,32,4096]{2,1,0:T(8,128)(2,1)}), bf16[8,32,4096]{2,1,0:T(8,128)(2,1)S(1)}, u32[]{:S(2)}, u32[]{:S(2)}) async-start(bf16[8,32,4096]{2,1,0:T(8,128)(2,1)} %bitcast.50), calls=%async_computation.1 | async-start | bytes 4194304 | tf_op jit(solution)/shard_map/all_to_all | solution.py:388
  94.4 102.1 %collective-permute-start.2 = (bf16[1,512,4096]{2,1,0:T(8,128)(2,1)}, bf16[1,512,4096]{2,1,0:T(8,128)(2,1)}, u32[]{:S(2)}, u32[]{:S(2)}) collective-permute-start(bf16[1,512,4096]{2,1,0:T(8,128)(2,1)} %refs_12_.1), channel_id=1, source_target_pairs={{0,8},{8,0},{1,9},{9,1},{2,10},{10,2},{3,11},{11,3},{4,12},{12,4},... | collective-permute-start | bytes 12582920 | tf_op jit(solution)/shard_map/ppermute | solution.py:28
  94.4 104.0 %collective-permute-start.3 = (bf16[1,512,4096]{2,1,0:T(8,128)(2,1)}, bf16[1,512,4096]{2,1,0:T(8,128)(2,1)}, u32[]{:S(2)}, u32[]{:S(2)}) collective-permute-start(bf16[1,512,4096]{2,1,0:T(8,128)(2,1)} %refs_13_.1), channel_id=1, source_target_pairs={{0,8},{8,0},{1,9},{9,1},{2,10},{10,2},{3,11},{11,3},{4,12},{12,4},... | collective-permute-start | bytes 12582920 | tf_op jit(solution)/shard_map/ppermute | solution.py:28
  120.8 15.8 %all-to-all-start.2 = ((bf16[8,24,2048]{2,1,0:T(8,128)(2,1)}), bf16[8,24,2048]{2,1,0:T(8,128)(2,1)S(1)}, u32[]{:S(2)}, u32[]{:S(2)}) async-start(bf16[8,24,2048]{2,1,0:T(8,128)(2,1)} %bitcast.12), calls=%async_computation.2 | async-start | bytes 1572864 | tf_op jit(solution)/shard_map/all_to_all | solution.py:412
  124.4 109.9 %collective-permute-start.16 = (bf16[1,512,4096]{2,1,0:T(8,128)(2,1)}, bf16[1,512,4096]{2,1,0:T(8,128)(2,1)}, u32[]{:S(2)}, u32[]{:S(2)}) collective-permute-start(bf16[1,512,4096]{2,1,0:T(8,128)(2,1)} %refs_2_.3), channel_id=1, source_target_pairs={{0,8},{8,0},{1,9},{9,1},{2,10},{10,2},{3,11},{11,3},{4,12},{12,4},... | collective-permute-start | bytes 12582920 | tf_op jit(solution)/shard_map/ppermute | solution.py:28
  124.5 14.5 %collective-permute-start.29 = (bf16[2,256,128]{2,1,0:T(8,128)(2,1)S(1)}, bf16[2,256,128]{2,1,0:T(8,128)(2,1)S(1)}, u32[]{:S(2)}, u32[]{:S(2)}) collective-permute-start(bf16[2,256,128]{2,1,0:T(8,128)(2,1)S(1)} %copy-done.9), channel_id=1, source_target_pairs={{0,8},{8,0},{1,9},{9,1},{2,10},{10,2},{3,11},{11,3},{4,12},{12,4},... | collective-permute-start | bytes 393224 | tf_op jit(solution)/shard_map/ppermute | solution.py:28
  136.8 13.7 %collective-permute-start = (bf16[96,2048]{1,0:T(8,128)(2,1)S(1)}, bf16[96,2048]{1,0:T(8,128)(2,1)}, u32[]{:S(2)}, u32[]{:S(2)}) collective-permute-start(bf16[96,2048]{1,0:T(8,128)(2,1)S(1)} %reshape.337.refs_0_), channel_id=1, source_target_pairs={{0,16},{16,0},{1,17},{17,1},{2,18},{18,2},{3,19},{19,3},{4,20},{20... | collective-permute-start | bytes 1179656 | tf_op jit(solution)/shard_map/ppermute | solution.py:28
  139.0 18.2 %collective-permute-start.1 = (bf16[96,2048]{1,0:T(8,128)(2,1)S(1)}, bf16[96,2048]{1,0:T(8,128)(2,1)}, u32[]{:S(2)}, u32[]{:S(2)}) collective-permute-start(bf16[96,2048]{1,0:T(8,128)(2,1)S(1)} %reshape.338.refs_2_), channel_id=1, source_target_pairs={{0,16},{16,0},{1,17},{17,1},{2,18},{18,2},{3,19},{19,3},{4,20},{20... | collective-permute-start | bytes 1179656 | tf_op jit(solution)/shard_map/ppermute | solution.py:28
  183.3 32.5 %collective-permute-start.12 = (bf16[192,2048]{1,0:T(8,128)(2,1)}, bf16[192,2048]{1,0:T(8,128)(2,1)}, u32[]{:S(2)}, u32[]{:S(2)}) collective-permute-start(bf16[192,2048]{1,0:T(8,128)(2,1)} %pad_maximum_fusion.1), channel_id=1, source_target_pairs={{0,16},{16,0},{1,17},{17,1},{2,18},{18,2},{3,19},{19,3},{4,20},{20... | collective-permute-start | bytes 2359304 | tf_op jit(solution)/shard_map/ppermute | solution.py:28
  196.4 17.6 %collective-permute-start.8 = (bf16[96,2048]{1,0:T(8,128)(2,1)}, bf16[96,2048]{1,0:T(8,128)(2,1)S(1)}, u32[]{:S(2)}, u32[]{:S(2)}) collective-permute-start(bf16[96,2048]{1,0:T(8,128)(2,1)} %copy-done.15), channel_id=1, source_target_pairs={{0,32},{32,64},{64,96},{96,0},{1,33},{33,65},{65,97},{97,1},{2,34}... | collective-permute-start | bytes 1179656 | tf_op jit(solution)/shard_map/ppermute | solution.py:24
  196.5 19.3 %collective-permute-start.15 = (bf16[96,2048]{1,0:T(8,128)(2,1)S(1)}, bf16[96,2048]{1,0:T(8,128)(2,1)S(1)}, u32[]{:S(2)}, u32[]{:S(2)}) collective-permute-start(bf16[96,2048]{1,0:T(8,128)(2,1)S(1)} %pad_maximum_fusion.5), channel_id=1, source_target_pairs={{0,16},{16,0},{1,17},{17,1},{2,18},{18,2},{3,19},{19,3},{4,20},{20... | collective-permute-start | bytes 1179656 | tf_op jit(solution)/shard_map/ppermute | solution.py:28
  198.5 17.3 %collective-permute-start.9 = (bf16[96,2048]{1,0:T(8,128)(2,1)}, bf16[96,2048]{1,0:T(8,128)(2,1)S(1)}, u32[]{:S(2)}, u32[]{:S(2)}) collective-permute-start(bf16[96,2048]{1,0:T(8,128)(2,1)} %collective-permute-done.7.refs_3_), channel_id=1, source_target_pairs={{0,96},{32,0},{64,32},{96,64},{1,97},{33,1},{65,33},{97,65},{2,98}... | collective-permute-start | bytes 1179656 | tf_op jit(solution)/shard_map/ppermute | solution.py:24
  214.1 29.1 %collective-permute-start.30 = (bf16[2,2,256,128]{3,2,1,0:T(8,128)(2,1)S(1)}, bf16[2,2,256,128]{3,2,1,0:T(8,128)(2,1)S(1)}, u32[]{:S(2)}, u32[]{:S(2)}) collective-permute-start(bf16[2,2,256,128]{3,2,1,0:T(8,128)(2,1)S(1)} %pad_maximum_fusion.8), channel_id=1, source_target_pairs={{0,16},{16,0},{1,17},{17,1},{2,18},{18,2},{3,19},{19,3},{4,20},{20... | collective-permute-start | bytes 786440 | tf_op jit(solution)/shard_map/ppermute | solution.py:28
  243.2 81.5 %collective-permute-start.31 = (bf16[4,2,256,128]{3,2,1,0:T(8,128)(2,1)S(1)}, bf16[4,2,256,128]{3,2,1,0:T(8,128)(2,1)}, u32[]{:S(2)}, u32[]{:S(2)}) collective-permute-start(bf16[4,2,256,128]{3,2,1,0:T(8,128)(2,1)S(1)} %pad_maximum_fusion.4.refs_0_), channel_id=1, source_target_pairs={{0,32},{32,64},{64,96},{96,0},{1,33},{33,65},{65,97},{97,1},{2,34}... | collective-permute-start | bytes 1572872 | tf_op jit(solution)/shard_map/ppermute | solution.py:24
  243.3 81.4 %collective-permute-start.32 = (bf16[4,2,256,128]{3,2,1,0:T(8,128)(2,1)S(1)}, bf16[4,2,256,128]{3,2,1,0:T(8,128)(2,1)}, u32[]{:S(2)}, u32[]{:S(2)}) collective-permute-start(bf16[4,2,256,128]{3,2,1,0:T(8,128)(2,1)S(1)} %pad_maximum_fusion.4.refs_0_), channel_id=1, source_target_pairs={{0,64},{32,96},{64,0},{96,32},{1,65},{33,97},{65,1},{97,33},{2,66}... | collective-permute-start | bytes 1572872 | tf_op jit(solution)/shard_map/ppermute | solution.py:24
  246.7 30.4 %collective-permute-start.23 = (bf16[192,2048]{1,0:T(8,128)(2,1)S(1)}, bf16[192,2048]{1,0:T(8,128)(2,1)S(1)}, u32[]{:S(2)}, u32[]{:S(2)}) collective-permute-start(bf16[192,2048]{1,0:T(8,128)(2,1)S(1)} %get-tuple-element.37), channel_id=1, source_target_pairs={{0,16},{16,0},{1,17},{17,1},{2,18},{18,2},{3,19},{19,3},{4,20},{20... | collective-permute-start | bytes 2359304 | tf_op jit(solution)/shard_map/ppermute | solution.py:28
  253.6 19.8 %collective-permute-start.19 = (bf16[96,2048]{1,0:T(8,128)(2,1)S(1)}, bf16[96,2048]{1,0:T(8,128)(2,1)S(1)}, u32[]{:S(2)}, u32[]{:S(2)}) collective-permute-start(bf16[96,2048]{1,0:T(8,128)(2,1)S(1)} %get-tuple-element.33), channel_id=1, source_target_pairs={{0,32},{32,64},{64,96},{96,0},{1,33},{33,65},{65,97},{97,1},{2,34}... | collective-permute-start | bytes 1179656 | tf_op jit(solution)/shard_map/ppermute | solution.py:24
  254.6 18.9 %collective-permute-start.17 = (bf16[96,2048]{1,0:T(8,128)(2,1)S(1)}, bf16[96,2048]{1,0:T(8,128)(2,1)S(1)}, u32[]{:S(2)}, u32[]{:S(2)}) collective-permute-start(bf16[96,2048]{1,0:T(8,128)(2,1)S(1)} %get-tuple-element.29), channel_id=1, source_target_pairs={{0,96},{32,0},{64,32},{96,64},{1,97},{33,1},{65,33},{97,65},{2,98}... | collective-permute-start | bytes 1179656 | tf_op jit(solution)/shard_map/ppermute | solution.py:24
  277.0 18.5 %collective-permute-start.20 = (bf16[192,2048]{1,0:T(8,128)(2,1)S(1)}, bf16[192,2048]{1,0:T(8,128)(2,1)S(1)}, u32[]{:S(2)}, u32[]{:S(2)}) collective-permute-start(bf16[192,2048]{1,0:T(8,128)(2,1)S(1)} %pad_maximum_fusion.3), channel_id=1, source_target_pairs={{0,32},{32,64},{64,96},{96,0},{1,33},{33,65},{65,97},{97,1},{2,34}... | collective-permute-start | bytes 2359304 | tf_op jit(solution)/shard_map/ppermute | solution.py:24
  282.3 15.4 %collective-permute-start.18 = (bf16[192,2048]{1,0:T(8,128)(2,1)S(1)}, bf16[192,2048]{1,0:T(8,128)(2,1)S(1)}, u32[]{:S(2)}, u32[]{:S(2)}) collective-permute-start(bf16[192,2048]{1,0:T(8,128)(2,1)S(1)} %pad_maximum_fusion.2), channel_id=1, source_target_pairs={{0,96},{32,0},{64,32},{96,64},{1,97},{33,1},{65,33},{97,65},{2,98}... | collective-permute-start | bytes 2359304 | tf_op jit(solution)/shard_map/ppermute | solution.py:24
  284.2 15.8 %collective-permute-start.22 = (bf16[96,2048]{1,0:T(8,128)(2,1)S(1)}, bf16[96,2048]{1,0:T(8,128)(2,1)S(1)}, u32[]{:S(2)}, u32[]{:S(2)}) collective-permute-start(bf16[96,2048]{1,0:T(8,128)(2,1)S(1)} %get-tuple-element.35), channel_id=1, source_target_pairs={{0,16},{16,0},{1,17},{17,1},{2,18},{18,2},{3,19},{19,3},{4,20},{20... | collective-permute-start | bytes 1179656 | tf_op jit(solution)/shard_map/ppermute | solution.py:28
  300.0 24.7 %collective-permute-start.33 = (bf16[4,2,256,128]{3,2,1,0:T(8,128)(2,1)S(1)}, bf16[4,2,256,128]{3,2,1,0:T(8,128)(2,1)}, u32[]{:S(2)}, u32[]{:S(2)}) collective-permute-start(bf16[4,2,256,128]{3,2,1,0:T(8,128)(2,1)S(1)} %pad_maximum_fusion.4.refs_0_), channel_id=1, source_target_pairs={{0,96},{32,0},{64,32},{96,64},{1,97},{33,1},{65,33},{97,65},{2,98}... | collective-permute-start | bytes 1572872 | tf_op jit(solution)/shard_map/ppermute | solution.py:24
  318.9 14.2 %all-to-all-start.3 = ((bf16[8,24,2048]{2,1,0:T(8,128)(2,1)}), bf16[8,24,2048]{2,1,0:T(8,128)(2,1)S(1)}, u32[]{:S(2)}, u32[]{:S(2)}) async-start(bf16[8,24,2048]{2,1,0:T(8,128)(2,1)} %copy.88), calls=%async_computation.3 | async-start | bytes 1572864 | tf_op jit(solution)/shard_map/all_to_all | solution.py:492
  (36 other events, 574.2 us)

commit v2 on v1

--- a/solution.py
+++ b/solution.py
@@ -284,7 +284,7 @@
             pltpu.VMEM((rows, width), jnp.bfloat16),
             pltpu.SemaphoreType.DMA((sum(len(m[0]) for m in moves),)),
         ],
-        compiler_params=pltpu.CompilerParams(vmem_limit_bytes=56_000_000),
+        compiler_params=pltpu.CompilerParams(vmem_limit_bytes=48_500_000),
         cost_estimate=pl.CostEstimate(
             flops=8 * rows * units * width,
             bytes_accessed=8 * units * width + 2 * rows * width,
@@ -297,37 +297,49 @@
 def down_body(moves, n_in, *refs):
     ins, (own, other), outs = refs[:n_in], refs[n_in : n_in + 2], refs[n_in + 2 :]
     units = own.shape[1]
-    for of, ref in enumerate(ins):
+    step, steps = pl.program_id(0), pl.num_programs(0)
+    sums = []
+    for ref in ins:
         h = ref[...]
         y = jnp.dot(h[:, :units], own[0], preferred_element_type=jnp.float32)
         y += jnp.dot(h[:, units:], other[0], preferred_element_type=jnp.float32)
-        y = y.astype(jnp.bfloat16)
-        for out, places in zip(outs, moves):
-            n = out.shape[0] // len(places)
-            for i, (source, r) in enumerate(places):
-                if source == of:
-                    out[i * n : (i + 1) * n] = y[r : r + n]
-
-
-def down_sums(hidden, own, other, start, size, shapes_out, tile=512):
-    _, units, _ = own[2].shape
-    weight = pl.BlockSpec((1, units, tile), lambda i: (0, 0, start // tile + i))
-    rows, moves = zip(*shapes_out)
-    total = sum(h.shape[0] for h in hidden)
+        sums.append(y.astype(jnp.bfloat16))
+    for part, here in enumerate((step < steps // 2, step >= steps // 2)):
+
+        @pl.when(here)
+        def _(part=part):
+            for out, (of, places) in zip(outs, moves):
+                n = out.shape[0] // len(places)
+                for i, (source, r) in enumerate(places):
+                    if of == part:
+                        out[i * n : (i + 1) * n] = sums[source][r : r + n]
+
+
+def down_sums(hidden, own, other, shapes_out, tile=1024):
+    _, units, width = own[2].shape
+    half = width // 2 // tile
+    weight = pl.BlockSpec((1, units, tile), lambda i: (0, 0, i))
+    columns = (lambda i: (0, jnp.minimum(i, half - 1)), lambda i: (0, jnp.maximum(i - half, 0)))
+    moves = tuple((part, places) for part, _, places in shapes_out)
+    total = sum(rows for _, rows, _ in hidden)
     return pl.pallas_call(
         functools.partial(down_body, moves, len(hidden)),
-        grid=(size // tile,),
-        in_specs=[pl.BlockSpec(h.shape, lambda i: (0, 0)) for h in hidden] + [weight, weight],
-        out_specs=[pl.BlockSpec((n, tile), lambda i: (0, i)) for n in rows],
-        out_shape=[jax.ShapeDtypeStruct((n, size), jnp.bfloat16) for n in rows],
-        compiler_params=pltpu.CompilerParams(vmem_limit_bytes=40_000_000),
+        grid=(2 * half,),
+        in_specs=[
+            pl.BlockSpec((rows, 2 * units), functools.partial(lambda at, i: (at, 0), at))
+            for _, rows, at in hidden
+        ]
+        + [weight, weight],
+        out_specs=[pl.BlockSpec((n, tile), columns[part]) for part, n, _ in shapes_out],
+        out_shape=[jax.ShapeDtypeStruct((n, width // 2), jnp.bfloat16) for _, n, _ in shapes_out],
+        compiler_params=pltpu.CompilerParams(vmem_limit_bytes=30_000_000),
         cost_estimate=pl.CostEstimate(
-            flops=4 * total * units * size,
-            bytes_accessed=4 * units * size + 2 * total * size + 4 * total * units,
+            flops=4 * total * units * width,
+            bytes_accessed=4 * units * width + 2 * total * width + 4 * total * units,
             transcendentals=0,
         ),
         name="down",
-    )(*hidden, own[2], other[2])
+    )(*[h for h, _, _ in hidden], own[2], other[2])
 
 
 def local(
@@ -447,23 +459,20 @@
         other,
         6 * n,
     )
-    o_b, r_b, l_b, f_b, x_o, x_rl, x_f = down_sums(
-        [h_o, h_r],
+    f1_a, f2_a, f_b, x_f = down_sums(
+        [(h_r, 2 * n, 2)],
         own,
         other,
-        w,
-        w,
-        [(n, ((0, 0),)), (n, ((1, 0),)), (n, ((1, 2 * n),)), (n, ((1, 4 * n),))]
-        + [(n, ((0, n),)), (2 * n, ((1, n), (1, 3 * n))), (n, ((1, 5 * n),))],
-    )
-    o_a, r_a, rx_a, l_a, lx_a, f1_a, f2_a = down_sums(
-        [h_o, h_r],
+        [(0, n, ((0, 0),)), (0, n, ((0, n),)), (1, n, ((0, 0),)), (1, n, ((0, n),))],
+    )
+    o_a, r_a, rx_a, l_a, lx_a, o_b, r_b, l_b, x_o, x_rl = down_sums(
+        [(h_o, 2 * n, 0), (h_r, 4 * n, 0)],
         own,
         other,
-        0,
-        w,
-        [(2 * n, ((0, 0),)), (n, ((1, 0),)), (n, ((1, n),)), (n, ((1, 2 * n),))]
-        + [(n, ((1, 3 * n),)), (n, ((1, 4 * n),)), (n, ((1, 5 * n),))],
+        [(0, 2 * n, ((0, 0),))]
+        + [(0, n, ((1, r),)) for r in (0, n, 2 * n, 3 * n)]
+        + [(1, n, ((0, 0),)), (1, n, ((1, 0),)), (1, n, ((1, 2 * n),)), (1, n, ((0, n),))]
+        + [(1, 2 * n, ((1, n), (1, 3 * n)))],
     )
 
     bf = jnp.bfloat16

time: 336 us -> 344 us (1.024)
  local copies, waits for them, and re-layouts: 12.3 us -> 17.8 us
  starting transfers between devices: 62.4 us -> 67.4 us
    ppermute x13, waiting for transfers between devices: 18.8 us -> 26.5 us  [swap(): return lax.ppermute(x, axis, [(0, 1), (1, 0)])]
    unnamed x46 -> x54, local copies, waits for them, and re-layouts: 3.69 us -> 8.87 us
    ppermute x21, waiting for transfers between devices: 68 us -> 62.9 us  [shift_z(): return lax.ppermute(x, 'z', [(i, (i + by) % n) for i in range(n)])]
    ppermute x21, starting transfers between devices: 24.5 us -> 28.8 us  [shift_z(): return lax.ppermute(x, 'z', [(i, (i + by) % n) for i in range(n)])]
    pallas_call x2, Pallas kernels: 29.9 us -> 26.2 us  [hidden_units(): pl.pallas_call(functools.partial(hidden_body, moves), grid=(2 * half,), i...]
  transfers between devices with their start and end apart: 38 -> 38, of which waited for: 21 -> 22; matrix products, arithmetic and copies ran while one was open for 6% -> 6% of each run, Pallas kernels for 13% -> 12%
where the time goes in v2:
time: 344 us; the launch traced here: 343 us
  waiting for transfers between devices  174 us (51%)
  starting transfers between devices  67.4 us (20%)
  Pallas kernels  63.7 us (19%)
  local copies, waits for them, and re-layouts  17.8 us (5%)
  other arithmetic  12.3 us (4%)
  matrix products  6.63 us (2%)
    ppermute x21, waiting for transfers between devices, shift_z(): return lax.ppermute(x, 'z', [(i, (i + by) % n) for i in range(n)])  62.9 us
    all_to_all x1, waiting for transfers between devices, local(): lax.all_to_all(outgoing, GROUP, split_axis=0, concat_axis=0, tiled=True)  49.2 us
    ppermute x21, starting transfers between devices, shift_z(): return lax.ppermute(x, 'z', [(i, (i + by) % n) for i in range(n)])  28.8 us
    ppermute x13, waiting for transfers between devices, swap(): return lax.ppermute(x, axis, [(0, 1), (1, 0)])  26.5 us
    pallas_call x2, Pallas kernels, hidden_units(): pl.pallas_call(functools.partial(hidden_body, moves), grid=(2 * half,), i...  26.2 us
    all_to_all x1, waiting for transfers between devices, local(): lax.all_to_all(partial, TENSOR, split_axis=0, concat_axis=0, tiled=True)  23.4 us
    pallas_call x1, Pallas kernels, attention(): pl.pallas_call(functools.partial(attend_body, begin, end, per), grid_spec...  17.5 us
    ppermute x13, starting transfers between devices, swap(): return lax.ppermute(x, axis, [(0, 1), (1, 0)])  17.5 us
  transfers between devices with their start and end apart: 38, of which 22 were waited for; matrix products, arithmetic and copies ran while one was open for 6% of the time, Pallas kernels for 12%

profile of v2, /device:TPU:0, one launch (start us, length us, event | category | flops | bytes accessed | tf_op | source)
XLA Modules:
  0.0 343.4 jit_solution(92152162042312597)
XLA Ops:
  2.0 4.2 %select.152 = bf16[16,2,512,128]{3,2,1,0:T(8,128)(2,1)} custom-call(s32[16]{0:T(128)} %fusion.18.picked, f32[2,1,4]{2,1,0:T(1,128)} %bitcast.60, bf16[2,4,512,128]{3,2,1,0:T(8,128)(2,1)} %bitcast.51), custom_call_target="tpu_custom_call" | custom-call | flops 1048576 | bytes 6291456 | tf_op jit(solution)/shard_map/select/pallas_call | solution.py:67
  6.3 8.1 %all-to-all-start = ((bf16[16,2,512,128]{3,2,1,0:T(8,128)(2,1)}), bf16[16,2,512,128]{3,2,1,0:T(8,128)(2,1)}, u32[]{:S(2)}, u32[]{:S(2)}) async-start(bf16[16,2,512,128]{3,2,1,0:T(8,128)(2,1)} %select.152), calls=%async_computation | async-start | bytes 8388608 | tf_op jit(solution)/shard_map/all_to_all | solution.py:380
  16.9 49.2 %all-to-all-done.kv_ref = bf16[16,2,512,128]{3,2,1,0:T(8,128)(2,1)} async-done(((bf16[16,2,512,128]{3,2,1,0:T(8,128)(2,1)}), bf16[16,2,512,128]{3,2,1,0:T(8,128)(2,1)}, u32[]{:S(2)}, u32[]{:S(2)}) %all-to-all-start) | async-done | bytes 4194336 | tf_op jit(solution)/shard_map/all_to_all | solution.py:380
  66.1 17.5 %attend.1 = bf16[256,512]{1,0:T(8,128)(2,1)} custom-call(s32[16]{0:T(128)} %convert_element_type.115.live, bf16[256,512]{1,0:T(8,128)(2,1)} %q_ref.1, bf16[2,256,128]{2,1,0:T(8,128)(2,1)} %new_ref.1, bf16[16,2,512,128]{3,2,1,0:T(8,128)(2,1)} %all-to-all-done.kv_ref), custom_call_target="tpu_custom_call" | custom-call | flops 6442450944 | bytes 5242880 | tf_op jit(solution)/shard_map/attend/pallas_call | solution.py:170
  83.6 4.8 %convolution_convert_fusion = bf16[256,4096]{1,0:T(8,128)(2,1)} fusion(bf16[256,512]{1,0:T(8,128)(2,1)} %attend.1, bf16[512,4096]{1,0:T(8,128)(2,1)} %param.22), kind=kOutput, calls=%fused_computation | convolution fusion | flops 1074790400 | bytes 6553600 | tf_op jit(solution)/shard_map/dot_general | solution.py:398
  88.5 4.6 %all-to-all-start.1 = ((bf16[8,32,4096]{2,1,0:T(8,128)(2,1)}), bf16[8,32,4096]{2,1,0:T(8,128)(2,1)S(1)}, u32[]{:S(2)}, u32[]{:S(2)}) async-start(bf16[8,32,4096]{2,1,0:T(8,128)(2,1)} %bitcast.50), calls=%async_computation.1 | async-start | bytes 4194304 | tf_op jit(solution)/shard_map/all_to_all | solution.py:400
  95.4 23.4 %all-to-all-done.1 = bf16[8,32,4096]{2,1,0:T(8,128)(2,1)S(1)} async-done(((bf16[8,32,4096]{2,1,0:T(8,128)(2,1)}), bf16[8,32,4096]{2,1,0:T(8,128)(2,1)S(1)}, u32[]{:S(2)}, u32[]{:S(2)}) %all-to-all-start.1) | async-done | bytes 2097184 | tf_op jit(solution)/shard_map/all_to_all | solution.py:400
  128.5 8.7 %all-to-all-done.2 = bf16[8,24,2048]{2,1,0:T(8,128)(2,1)S(1)} async-done(((bf16[8,24,2048]{2,1,0:T(8,128)(2,1)}), bf16[8,24,2048]{2,1,0:T(8,128)(2,1)S(1)}, u32[]{:S(2)}, u32[]{:S(2)}) %all-to-all-start.2) | async-done | bytes 786464 | tf_op jit(solution)/shard_map/all_to_all | solution.py:424
  142.9 7.4 %collective-permute-done.refs_1_ = bf16[96,2048]{1,0:T(8,128)(2,1)S(1)} collective-permute-done((bf16[96,2048]{1,0:T(8,128)(2,1)S(1)}, bf16[96,2048]{1,0:T(8,128)(2,1)S(1)}, u32[]{:S(2)}, u32[]{:S(2)}) %collective-permute-start) | collective-permute-done | bytes 393248 | tf_op jit(solution)/shard_map/ppermute | solution.py:28
  153.5 8.1 %collective-permute-done.10.refs_6_ = bf16[96,2048]{1,0:T(8,128)(2,1)S(1)} collective-permute-done((bf16[96,2048]{1,0:T(8,128)(2,1)S(1)}, bf16[96,2048]{1,0:T(8,128)(2,1)S(1)}, u32[]{:S(2)}, u32[]{:S(2)}) %collective-permute-start.10) | collective-permute-done | bytes 393248 | tf_op jit(solution)/shard_map/ppermute | solution.py:24
  164.5 6.5 %collective-permute-done.11.refs_7_ = bf16[96,2048]{1,0:T(8,128)(2,1)S(1)} collective-permute-done((bf16[96,2048]{1,0:T(8,128)(2,1)S(1)}, bf16[96,2048]{1,0:T(8,128)(2,1)S(1)}, u32[]{:S(2)}, u32[]{:S(2)}) %collective-permute-start.11) | collective-permute-done | bytes 393248 | tf_op jit(solution)/shard_map/ppermute | solution.py:24
  181.6 5.2 %collective-permute-done.7.refs_3_ = bf16[96,2048]{1,0:T(8,128)(2,1)} collective-permute-done((bf16[96,2048]{1,0:T(8,128)(2,1)S(1)}, bf16[96,2048]{1,0:T(8,128)(2,1)}, u32[]{:S(2)}, u32[]{:S(2)}) %collective-permute-start.7) | collective-permute-done | bytes 393248 | tf_op jit(solution)/shard_map/ppermute | solution.py:24
  192.8 7.5 %collective-permute-done.15.refs_11_ = bf16[96,2048]{1,0:T(8,128)(2,1)S(1)} collective-permute-done((bf16[96,2048]{1,0:T(8,128)(2,1)S(1)}, bf16[96,2048]{1,0:T(8,128)(2,1)S(1)}, u32[]{:S(2)}, u32[]{:S(2)}) %collective-permute-start.15) | collective-permute-done | bytes 393248 | tf_op jit(solution)/shard_map/ppermute | solution.py:28
  216.2 5.1 %collective-permute-start.32 = (bf16[4,2,256,128]{3,2,1,0:T(8,128)(2,1)}, bf16[4,2,256,128]{3,2,1,0:T(8,128)(2,1)}, u32[]{:S(2)}, u32[]{:S(2)}) collective-permute-start(bf16[4,2,256,128]{3,2,1,0:T(8,128)(2,1)} %pad_maximum_fusion.4.refs_0_), channel_id=1, source_target_pairs={{0,64},{32,96},{64,0},{96,32},{1,65},{33,97},{65,1},{97,33},{2,66}... | collective-permute-start | bytes 1572872 | tf_op jit(solution)/shard_map/ppermute | solution.py:24
  226.8 16.2 %hidden.3.refs_1_.refs_0_ = bf16[576,1024]{1,0:T(8,128)(2,1)S(1)} custom-call(bf16[96,2048]{1,0:T(8,128)(2,1)S(1)} %collective-permute-done.4.refs_0_, bf16[96,2048]{1,0:T(8,128)(2,1)S(1)} %copy-done.5, bf16[96,2048]{1,0:T(8,128)(2,1)S(1)} %copy-done.3, bf16[96,2048]{1,0:T(8,128)(2,1)} %collective-permute-done.7.refs_3_, bf16[96,2048]{1,0:T(8,128)(2,1)S(1)} %copy-done.7, ...), custom_call_target="tpu_custom_call" | custom-call | flops 9663676416 | bytes 21495808 | tf_op jit(solution)/shard_map/hidden/pallas_call | solution.py:277
  243.0 5.0 %down.3 = (bf16[96,2048]{1,0:T(8,128)(2,1)S(1)}, bf16[96,2048]{1,0:T(8,128)(2,1)S(1)}, bf16[96,2048]{1,0:T(8,128)(2,1)S(1)}, bf16[96,2048]{1,0:T(8,128)(2,1)S(1)}) custom-call(bf16[576,1024]{1,0:T(8,128)(2,1)S(1)} %hidden.3.refs_1_.refs_0_, bf16[1,512,4096]{2,1,0:T(8,128)(2,1)S(1)} %copy-done, bf16[1,512,4096]{2,1,0:T(8,128)(2,1)} %collective-permute-done.16.refs_3_.refs_2_), custom_call_target="tpu_custom_call" | custom-call | flops 1610612736 | bytes 10354688 | tf_op jit(solution)/shard_map/down/pallas_call | solution.py:325
  250.1 10.0 %hidden.2.refs_0_ = bf16[192,1024]{1,0:T(8,128)(2,1)S(1)} custom-call(bf16[96,2048]{1,0:T(8,128)(2,1)S(1)} %reshape.337.refs_0_, bf16[96,2048]{1,0:T(8,128)(2,1)S(1)} %collective-permute-done.refs_1_, bf16[96,2048]{1,0:T(8,128)(2,1)S(1)} %reshape.338.refs_2_, bf16[96,2048]{1,0:T(8,128)(2,1)S(1)} %collective-permute-done.1.refs_3_, ...), custom_call_target="tpu_custom_call" | custom-call | flops 3221225472 | bytes 18350080 | tf_op jit(solution)/shard_map/hidden/pallas_call | solution.py:277
  260.1 8.2 %down.2 = (bf16[192,2048]{1,0:T(8,128)(2,1)S(1)}, bf16[96,2048]{1,0:T(8,128)(2,1)S(1)}, bf16[96,2048]{1,0:T(8,128)(2,1)S(1)}, bf16[96,2048]{1,0:T(8,128)(2,1)S(1...) custom-call(bf16[192,1024]{1,0:T(8,128)(2,1)S(1)} %hidden.2.refs_0_,, ...), custom_call_target="tpu_custom_call" | custom-call | flops 4831838208 | bytes 14286848 | tf_op jit(solution)/shard_map/down/pallas_call | solution.py:325
  273.5 9.8 %collective-permute-done.19 = bf16[96,2048]{1,0:T(8,128)(2,1)S(1)} collective-permute-done((bf16[96,2048]{1,0:T(8,128)(2,1)S(1)}, bf16[96,2048]{1,0:T(8,128)(2,1)S(1)}, u32[]{:S(2)}, u32[]{:S(2)}) %collective-permute-start.19) | collective-permute-done | bytes 393248 | tf_op jit(solution)/shard_map/ppermute | solution.py:24
  287.3 4.4 %collective-permute-done.27 = bf16[96,1024]{1,0:T(8,128)(2,1)S(1)} collective-permute-done((bf16[96,1024]{1,0:T(8,128)(2,1)S(1)}, bf16[96,1024]{1,0:T(8,128)(2,1)S(1)}, u32[]{:S(2)}, u32[]{:S(2)}) %collective-permute-start.27) | collective-permute-done | bytes 196640 | tf_op jit(solution)/shard_map/ppermute | solution.py:24
  294.2 8.7 %collective-permute-done.20 = bf16[192,2048]{1,0:T(8,128)(2,1)S(1)} collective-permute-done((bf16[192,2048]{1,0:T(8,128)(2,1)S(1)}, bf16[192,2048]{1,0:T(8,128)(2,1)S(1)}, u32[]{:S(2)}, u32[]{:S(2)}) %collective-permute-start.20) | collective-permute-done | bytes 786464 | tf_op jit(solution)/shard_map/ppermute | solution.py:24
  302.9 5.4 %collective-permute-done.18 = bf16[192,2048]{1,0:T(8,128)(2,1)S(1)} collective-permute-done((bf16[192,2048]{1,0:T(8,128)(2,1)S(1)}, bf16[192,2048]{1,0:T(8,128)(2,1)S(1)}, u32[]{:S(2)}, u32[]{:S(2)}) %collective-permute-start.18) | collective-permute-done | bytes 786464 | tf_op jit(solution)/shard_map/ppermute | solution.py:24
  317.6 6.9 %collective-permute-done.21 = bf16[96,2048]{1,0:T(8,128)(2,1)} collective-permute-done((bf16[96,2048]{1,0:T(8,128)(2,1)S(1)}, bf16[96,2048]{1,0:T(8,128)(2,1)}, u32[]{:S(2)}, u32[]{:S(2)}) %collective-permute-start.21) | collective-permute-done | bytes 393248 | tf_op jit(solution)/shard_map/ppermute | solution.py:28
  327.7 4.9 %all-to-all-start.3 = ((bf16[8,24,2048]{2,1,0:T(8,128)(2,1)}), bf16[8,24,2048]{2,1,0:T(8,128)(2,1)S(1)}, u32[]{:S(2)}, u32[]{:S(2)}) async-start(bf16[8,24,2048]{2,1,0:T(8,128)(2,1)} %copy.88), calls=%async_computation.3 | async-start | bytes 1572864 | tf_op jit(solution)/shard_map/all_to_all | solution.py:501
  (189 shorter events, 102.3 us)
Async XLA Ops:
  6.3 59.9 %all-to-all-start = ((bf16[16,2,512,128]{3,2,1,0:T(8,128)(2,1)}), bf16[16,2,512,128]{3,2,1,0:T(8,128)(2,1)}, u32[]{:S(2)}, u32[]{:S(2)}) async-start(bf16[16,2,512,128]{3,2,1,0:T(8,128)(2,1)} %select.152), calls=%async_computation | async-start | bytes 8388608 | tf_op jit(solution)/shard_map/all_to_all | solution.py:380
  88.5 30.3 %all-to-all-start.1 = ((bf16[8,32,4096]{2,1,0:T(8,128)(2,1)}), bf16[8,32,4096]{2,1,0:T(8,128)(2,1)S(1)}, u32[]{:S(2)}, u32[]{:S(2)}) async-start(bf16[8,32,4096]{2,1,0:T(8,128)(2,1)} %bitcast.50), calls=%async_computation.1 | async-start | bytes 4194304 | tf_op jit(solution)/shard_map/all_to_all | solution.py:400
  94.8 126.5 %collective-permute-start.2 = (bf16[1,512,4096]{2,1,0:T(8,128)(2,1)}, bf16[1,512,4096]{2,1,0:T(8,128)(2,1)}, u32[]{:S(2)}, u32[]{:S(2)}) collective-permute-start(bf16[1,512,4096]{2,1,0:T(8,128)(2,1)} %refs_12_.1), channel_id=1, source_target_pairs={{0,8},{8,0},{1,9},{9,1},{2,10},{10,2},{3,11},{11,3},{4,12},{12,4},... | collective-permute-start | bytes 12582920 | tf_op jit(solution)/shard_map/ppermute | solution.py:28
  94.9 127.9 %collective-permute-start.3 = (bf16[1,512,4096]{2,1,0:T(8,128)(2,1)}, bf16[1,512,4096]{2,1,0:T(8,128)(2,1)}, u32[]{:S(2)}, u32[]{:S(2)}) collective-permute-start(bf16[1,512,4096]{2,1,0:T(8,128)(2,1)} %refs_13_.1), channel_id=1, source_target_pairs={{0,8},{8,0},{1,9},{9,1},{2,10},{10,2},{3,11},{11,3},{4,12},{12,4},... | collective-permute-start | bytes 12582920 | tf_op jit(solution)/shard_map/ppermute | solution.py:28
  121.3 15.8 %all-to-all-start.2 = ((bf16[8,24,2048]{2,1,0:T(8,128)(2,1)}), bf16[8,24,2048]{2,1,0:T(8,128)(2,1)S(1)}, u32[]{:S(2)}, u32[]{:S(2)}) async-start(bf16[8,24,2048]{2,1,0:T(8,128)(2,1)} %bitcast.12), calls=%async_computation.2 | async-start | bytes 1572864 | tf_op jit(solution)/shard_map/all_to_all | solution.py:424
  126.4 16.4 %collective-permute-start.30 = (bf16[2,2,256,128]{3,2,1,0:T(8,128)(2,1)S(1)}, bf16[2,2,256,128]{3,2,1,0:T(8,128)(2,1)S(1)}, u32[]{:S(2)}, u32[]{:S(2)}) collective-permute-start(bf16[2,2,256,128]{3,2,1,0:T(8,128)(2,1)S(1)} %pad_maximum_fusion.8), channel_id=1, source_target_pairs={{0,16},{16,0},{1,17},{17,1},{2,18},{18,2},{3,19},{19,3},{4,20},{20... | collective-permute-start | bytes 786440 | tf_op jit(solution)/shard_map/ppermute | solution.py:28
  128.5 114.5 %collective-permute-start.16 = (bf16[1,512,4096]{2,1,0:T(8,128)(2,1)}, bf16[1,512,4096]{2,1,0:T(8,128)(2,1)}, u32[]{:S(2)}, u32[]{:S(2)}) collective-permute-start(bf16[1,512,4096]{2,1,0:T(8,128)(2,1)} %refs_1_.1), channel_id=1, source_target_pairs={{0,8},{8,0},{1,9},{9,1},{2,10},{10,2},{3,11},{11,3},{4,12},{12,4},... | collective-permute-start | bytes 12582920 | tf_op jit(solution)/shard_map/ppermute | solution.py:28
  137.4 12.9 %collective-permute-start = (bf16[96,2048]{1,0:T(8,128)(2,1)S(1)}, bf16[96,2048]{1,0:T(8,128)(2,1)S(1)}, u32[]{:S(2)}, u32[]{:S(2)}) collective-permute-start(bf16[96,2048]{1,0:T(8,128)(2,1)S(1)} %reshape.337.refs_0_), channel_id=1, source_target_pairs={{0,16},{16,0},{1,17},{17,1},{2,18},{18,2},{3,19},{19,3},{4,20},{20... | collective-permute-start | bytes 1179656 | tf_op jit(solution)/shard_map/ppermute | solution.py:28
  186.8 13.5 %collective-permute-start.15 = (bf16[96,2048]{1,0:T(8,128)(2,1)S(1)}, bf16[96,2048]{1,0:T(8,128)(2,1)S(1)}, u32[]{:S(2)}, u32[]{:S(2)}) collective-permute-start(bf16[96,2048]{1,0:T(8,128)(2,1)S(1)} %pad_maximum_fusion.5), channel_id=1, source_target_pairs={{0,16},{16,0},{1,17},{17,1},{2,18},{18,2},{3,19},{19,3},{4,20},{20... | collective-permute-start | bytes 1179656 | tf_op jit(solution)/shard_map/ppermute | solution.py:28
  191.3 24.9 %collective-permute-start.12 = (bf16[192,2048]{1,0:T(8,128)(2,1)}, bf16[192,2048]{1,0:T(8,128)(2,1)S(1)}, u32[]{:S(2)}, u32[]{:S(2)}) collective-permute-start(bf16[192,2048]{1,0:T(8,128)(2,1)} %pad_maximum_fusion.1), channel_id=1, source_target_pairs={{0,16},{16,0},{1,17},{17,1},{2,18},{18,2},{3,19},{19,3},{4,20},{20... | collective-permute-start | bytes 2359304 | tf_op jit(solution)/shard_map/ppermute | solution.py:28
  201.1 15.1 %collective-permute-start.9 = (bf16[96,2048]{1,0:T(8,128)(2,1)}, bf16[96,2048]{1,0:T(8,128)(2,1)}, u32[]{:S(2)}, u32[]{:S(2)}) collective-permute-start(bf16[96,2048]{1,0:T(8,128)(2,1)} %collective-permute-done.7.refs_3_), channel_id=1, source_target_pairs={{0,96},{32,0},{64,32},{96,64},{1,97},{33,1},{65,33},{97,65},{2,98}... | collective-permute-start | bytes 1179656 | tf_op jit(solution)/shard_map/ppermute | solution.py:24
  216.1 117.5 %collective-permute-start.31 = (bf16[4,2,256,128]{3,2,1,0:T(8,128)(2,1)}, bf16[4,2,256,128]{3,2,1,0:T(8,128)(2,1)}, u32[]{:S(2)}, u32[]{:S(2)}) collective-permute-start(bf16[4,2,256,128]{3,2,1,0:T(8,128)(2,1)} %pad_maximum_fusion.4.refs_0_), channel_id=1, source_target_pairs={{0,32},{32,64},{64,96},{96,0},{1,33},{33,65},{65,97},{97,1},{2,34}... | collective-permute-start | bytes 1572872 | tf_op jit(solution)/shard_map/ppermute | solution.py:24
  216.2 117.5 %collective-permute-start.32 = (bf16[4,2,256,128]{3,2,1,0:T(8,128)(2,1)}, bf16[4,2,256,128]{3,2,1,0:T(8,128)(2,1)}, u32[]{:S(2)}, u32[]{:S(2)}) collective-permute-start(bf16[4,2,256,128]{3,2,1,0:T(8,128)(2,1)} %pad_maximum_fusion.4.refs_0_), channel_id=1, source_target_pairs={{0,64},{32,96},{64,0},{96,32},{1,65},{33,97},{65,1},{97,33},{2,66}... | collective-permute-start | bytes 1572872 | tf_op jit(solution)/shard_map/ppermute | solution.py:24
  221.3 28.8 %collective-permute-start.1 = (bf16[96,2048]{1,0:T(8,128)(2,1)S(1)}, bf16[96,2048]{1,0:T(8,128)(2,1)S(1)}, u32[]{:S(2)}, u32[]{:S(2)}) collective-permute-start(bf16[96,2048]{1,0:T(8,128)(2,1)S(1)} %reshape.338.refs_2_), channel_id=1, source_target_pairs={{0,16},{16,0},{1,17},{17,1},{2,18},{18,2},{3,19},{19,3},{4,20},{20... | collective-permute-start | bytes 1179656 | tf_op jit(solution)/shard_map/ppermute | solution.py:28
  248.0 22.1 %collective-permute-start.24 = (bf16[96,2048]{1,0:T(8,128)(2,1)S(1)}, bf16[96,2048]{1,0:T(8,128)(2,1)S(1)}, u32[]{:S(2)}, u32[]{:S(2)}) collective-permute-start(bf16[96,2048]{1,0:T(8,128)(2,1)S(1)} %get-tuple-element.39), channel_id=1, source_target_pairs={{0,16},{16,0},{1,17},{17,1},{2,18},{18,2},{3,19},{19,3},{4,20},{20... | collective-permute-start | bytes 1179656 | tf_op jit(solution)/shard_map/ppermute | solution.py:28
  268.3 18.7 %collective-permute-start.23 = (bf16[192,2048]{1,0:T(8,128)(2,1)S(1)}, bf16[192,2048]{1,0:T(8,128)(2,1)S(1)}, u32[]{:S(2)}, u32[]{:S(2)}) collective-permute-start(bf16[192,2048]{1,0:T(8,128)(2,1)S(1)} %get-tuple-element.37), channel_id=1, source_target_pairs={{0,16},{16,0},{1,17},{17,1},{2,18},{18,2},{3,19},{19,3},{4,20},{20... | collective-permute-start | bytes 2359304 | tf_op jit(solution)/shard_map/ppermute | solution.py:28
  270.1 13.2 %collective-permute-start.19 = (bf16[96,2048]{1,0:T(8,128)(2,1)S(1)}, bf16[96,2048]{1,0:T(8,128)(2,1)S(1)}, u32[]{:S(2)}, u32[]{:S(2)}) collective-permute-start(bf16[96,2048]{1,0:T(8,128)(2,1)S(1)} %get-tuple-element.33), channel_id=1, source_target_pairs={{0,32},{32,64},{64,96},{96,0},{1,33},{33,65},{65,97},{97,1},{2,34}... | collective-permute-start | bytes 1179656 | tf_op jit(solution)/shard_map/ppermute | solution.py:24
  270.1 13.4 %collective-permute-start.17 = (bf16[96,2048]{1,0:T(8,128)(2,1)S(1)}, bf16[96,2048]{1,0:T(8,128)(2,1)S(1)}, u32[]{:S(2)}, u32[]{:S(2)}) collective-permute-start(bf16[96,2048]{1,0:T(8,128)(2,1)S(1)} %get-tuple-element.29), channel_id=1, source_target_pairs={{0,96},{32,0},{64,32},{96,64},{1,97},{33,1},{65,33},{97,65},{2,98}... | collective-permute-start | bytes 1179656 | tf_op jit(solution)/shard_map/ppermute | solution.py:24
  287.0 15.8 %collective-permute-start.20 = (bf16[192,2048]{1,0:T(8,128)(2,1)S(1)}, bf16[192,2048]{1,0:T(8,128)(2,1)S(1)}, u32[]{:S(2)}, u32[]{:S(2)}) collective-permute-start(bf16[192,2048]{1,0:T(8,128)(2,1)S(1)} %pad_maximum_fusion.3), channel_id=1, source_target_pairs={{0,32},{32,64},{64,96},{96,0},{1,33},{33,65},{65,97},{97,1},{2,34}... | collective-permute-start | bytes 2359304 | tf_op jit(solution)/shard_map/ppermute | solution.py:24
  291.7 16.6 %collective-permute-start.18 = (bf16[192,2048]{1,0:T(8,128)(2,1)S(1)}, bf16[192,2048]{1,0:T(8,128)(2,1)S(1)}, u32[]{:S(2)}, u32[]{:S(2)}) collective-permute-start(bf16[192,2048]{1,0:T(8,128)(2,1)S(1)} %pad_maximum_fusion.2), channel_id=1, source_target_pairs={{0,96},{32,0},{64,32},{96,64},{1,97},{33,1},{65,33},{97,65},{2,98}... | collective-permute-start | bytes 2359304 | tf_op jit(solution)/shard_map/ppermute | solution.py:24
  292.1 20.3 %collective-permute-start.22 = (bf16[96,2048]{1,0:T(8,128)(2,1)S(1)}, bf16[96,2048]{1,0:T(8,128)(2,1)S(1)}, u32[]{:S(2)}, u32[]{:S(2)}) collective-permute-start(bf16[96,2048]{1,0:T(8,128)(2,1)S(1)} %get-tuple-element.35), channel_id=1, source_target_pairs={{0,16},{16,0},{1,17},{17,1},{2,18},{18,2},{3,19},{19,3},{4,20},{20... | collective-permute-start | bytes 1179656 | tf_op jit(solution)/shard_map/ppermute | solution.py:28
  312.4 21.2 %collective-permute-start.33 = (bf16[4,2,256,128]{3,2,1,0:T(8,128)(2,1)}, bf16[4,2,256,128]{3,2,1,0:T(8,128)(2,1)S(1)}, u32[]{:S(2)}, u32[]{:S(2)}) collective-permute-start(bf16[4,2,256,128]{3,2,1,0:T(8,128)(2,1)} %pad_maximum_fusion.4.refs_0_), channel_id=1, source_target_pairs={{0,96},{32,0},{64,32},{96,64},{1,97},{33,1},{65,33},{97,65},{2,98}... | collective-permute-start | bytes 1572872 | tf_op jit(solution)/shard_map/ppermute | solution.py:24
  312.5 12.0 %collective-permute-start.21 = (bf16[96,2048]{1,0:T(8,128)(2,1)S(1)}, bf16[96,2048]{1,0:T(8,128)(2,1)}, u32[]{:S(2)}, u32[]{:S(2)}) collective-permute-start(bf16[96,2048]{1,0:T(8,128)(2,1)S(1)} %slice.116), channel_id=1, source_target_pairs={{0,16},{16,0},{1,17},{17,1},{2,18},{18,2},{3,19},{19,3},{4,20},{20... | collective-permute-start | bytes 1179656 | tf_op jit(solution)/shard_map/ppermute | solution.py:28
  327.7 14.3 %all-to-all-start.3 = ((bf16[8,24,2048]{2,1,0:T(8,128)(2,1)}), bf16[8,24,2048]{2,1,0:T(8,128)(2,1)S(1)}, u32[]{:S(2)}, u32[]{:S(2)}) async-start(bf16[8,24,2048]{2,1,0:T(8,128)(2,1)} %copy.88), calls=%async_computation.3 | async-start | bytes 1572864 | tf_op jit(solution)/shard_map/all_to_all | solution.py:501
  (40 other events, 336.1 us)

commit v3 on v2

--- a/solution.py
+++ b/solution.py
@@ -268,7 +268,7 @@
         run(*other)
 
 
-def hidden_units(pieces, own, other, rows, tile=256):
+def hidden_units(pieces, own, other, rows, limit, tile=256):
     _, units, width = own[0].shape
     half = units // tile
     first = pl.BlockSpec((1, tile, width), lambda i: (0, jnp.minimum(i, half - 1), 0))
@@ -284,7 +284,7 @@
             pltpu.VMEM((rows, width), jnp.bfloat16),
             pltpu.SemaphoreType.DMA((sum(len(m[0]) for m in moves),)),
         ],
-        compiler_params=pltpu.CompilerParams(vmem_limit_bytes=48_500_000),
+        compiler_params=pltpu.CompilerParams(vmem_limit_bytes=limit),
         cost_estimate=pl.CostEstimate(
             flops=8 * rows * units * width,
             bytes_accessed=8 * units * width + 2 * rows * width,
@@ -448,7 +448,7 @@
 
     w = half_width
     h_o = hidden_units(
-        [(a, ((0,), 0)), (ax, ((n,), 0)), (b, ((0,), w)), (bx, ((n,), w))], own, other, 2 * n
+        [(a, ((0,), 0)), (ax, ((n,), 0)), (b, ((0,), w)), (bx, ((n,), w))], own, other, 2 * n, 53_000_000
     )
     h_r = hidden_units(
         [(a_r, ((0,), 0)), (ax_r, ((n,), 0)), (a_l, ((2 * n,), 0)), (ax_l, ((3 * n,), 0))]
@@ -458,6 +458,7 @@
         own,
         other,
         6 * n,
+        48_500_000,
     )
     f1_a, f2_a, f_b, x_f = down_sums(
         [(h_r, 2 * n, 2)],

time: 344 us -> 345 us (level)
    unnamed x54 -> x52, local copies, waits for them, and re-layouts: 8.87 us -> 8.86 us
where the time goes in v3:
time: 345 us; the launch traced here: 344 us
  waiting for transfers between devices  174 us (50%)
  starting transfers between devices  67.5 us (20%)
  Pallas kernels  64.1 us (19%)
  local copies, waits for them, and re-layouts  17.7 us (5%)
  other arithmetic  12.3 us (4%)
  matrix products  6.64 us (2%)
    ppermute x21, waiting for transfers between devices, shift_z(): return lax.ppermute(x, 'z', [(i, (i + by) % n) for i in range(n)])  62.8 us
    all_to_all x1, waiting for transfers between devices, local(): lax.all_to_all(outgoing, GROUP, split_axis=0, concat_axis=0, tiled=True)  49.2 us
    ppermute x21, starting transfers between devices, shift_z(): return lax.ppermute(x, 'z', [(i, (i + by) % n) for i in range(n)])  28.8 us
    pallas_call x2, Pallas kernels, hidden_units(): pl.pallas_call(functools.partial(hidden_body, moves), grid=(2 * half,), i...  26.8 us
    ppermute x13, waiting for transfers between devices, swap(): return lax.ppermute(x, axis, [(0, 1), (1, 0)])  26.5 us
    all_to_all x1, waiting for transfers between devices, local(): lax.all_to_all(partial, TENSOR, split_axis=0, concat_axis=0, tiled=True)  23.4 us
    ppermute x13, starting transfers between devices, swap(): return lax.ppermute(x, axis, [(0, 1), (1, 0)])  17.5 us
    pallas_call x1, Pallas kernels, attention(): pl.pallas_call(functools.partial(attend_body, begin, end, per), grid_spec...  17.5 us
  transfers between devices with their start and end apart: 38, of which 22 were waited for; matrix products, arithmetic and copies ran while one was open for 6% of the time, Pallas kernels for 12%

profile of v3, /device:TPU:0, one launch (start us, length us, event | category | flops | bytes accessed | tf_op | source)
XLA Modules:
  0.0 343.7 jit_solution(2514924652142685730)
XLA Ops:
  6.3 8.1 %all-to-all-start = ((bf16[16,2,512,128]{3,2,1,0:T(8,128)(2,1)}), bf16[16,2,512,128]{3,2,1,0:T(8,128)(2,1)}, u32[]{:S(2)}, u32[]{:S(2)}) async-start(bf16[16,2,512,128]{3,2,1,0:T(8,128)(2,1)} %select.152), calls=%async_computation | async-start | bytes 8388608 | tf_op jit(solution)/shard_map/all_to_all | solution.py:380
  16.9 49.2 %all-to-all-done.kv_ref = bf16[16,2,512,128]{3,2,1,0:T(8,128)(2,1)} async-done(((bf16[16,2,512,128]{3,2,1,0:T(8,128)(2,1)}), bf16[16,2,512,128]{3,2,1,0:T(8,128)(2,1)}, u32[]{:S(2)}, u32[]{:S(2)}) %all-to-all-start) | async-done | bytes 4194336 | tf_op jit(solution)/shard_map/all_to_all | solution.py:380
  66.1 17.5 %attend.1 = bf16[256,512]{1,0:T(8,128)(2,1)} custom-call(s32[16]{0:T(128)} %convert_element_type.115.live, bf16[256,512]{1,0:T(8,128)(2,1)} %q_ref.1, bf16[2,256,128]{2,1,0:T(8,128)(2,1)} %new_ref.1, bf16[16,2,512,128]{3,2,1,0:T(8,128)(2,1)} %all-to-all-done.kv_ref), custom_call_target="tpu_custom_call" | custom-call | flops 6442450944 | bytes 5242880 | tf_op jit(solution)/shard_map/attend/pallas_call | solution.py:170
  83.6 4.9 %convolution_convert_fusion = bf16[256,4096]{1,0:T(8,128)(2,1)} fusion(bf16[256,512]{1,0:T(8,128)(2,1)} %attend.1, bf16[512,4096]{1,0:T(8,128)(2,1)} %param.22), kind=kOutput, calls=%fused_computation | convolution fusion | flops 1074790400 | bytes 6553600 | tf_op jit(solution)/shard_map/dot_general | solution.py:398
  88.5 4.6 %all-to-all-start.1 = ((bf16[8,32,4096]{2,1,0:T(8,128)(2,1)}), bf16[8,32,4096]{2,1,0:T(8,128)(2,1)S(1)}, u32[]{:S(2)}, u32[]{:S(2)}) async-start(bf16[8,32,4096]{2,1,0:T(8,128)(2,1)} %bitcast.50), calls=%async_computation.1 | async-start | bytes 4194304 | tf_op jit(solution)/shard_map/all_to_all | solution.py:400
  95.4 23.4 %all-to-all-done.1 = bf16[8,32,4096]{2,1,0:T(8,128)(2,1)S(1)} async-done(((bf16[8,32,4096]{2,1,0:T(8,128)(2,1)}), bf16[8,32,4096]{2,1,0:T(8,128)(2,1)S(1)}, u32[]{:S(2)}, u32[]{:S(2)}) %all-to-all-start.1) | async-done | bytes 2097184 | tf_op jit(solution)/shard_map/all_to_all | solution.py:400
  128.5 8.7 %all-to-all-done.2 = bf16[8,24,2048]{2,1,0:T(8,128)(2,1)S(1)} async-done(((bf16[8,24,2048]{2,1,0:T(8,128)(2,1)}), bf16[8,24,2048]{2,1,0:T(8,128)(2,1)S(1)}, u32[]{:S(2)}, u32[]{:S(2)}) %all-to-all-start.2) | async-done | bytes 786464 | tf_op jit(solution)/shard_map/all_to_all | solution.py:424
  142.9 7.4 %collective-permute-done.refs_1_ = bf16[96,2048]{1,0:T(8,128)(2,1)S(1)} collective-permute-done((bf16[96,2048]{1,0:T(8,128)(2,1)S(1)}, bf16[96,2048]{1,0:T(8,128)(2,1)S(1)}, u32[]{:S(2)}, u32[]{:S(2)}) %collective-permute-start) | collective-permute-done | bytes 393248 | tf_op jit(solution)/shard_map/ppermute | solution.py:28
  153.5 8.1 %collective-permute-done.10.refs_6_ = bf16[96,2048]{1,0:T(8,128)(2,1)S(1)} collective-permute-done((bf16[96,2048]{1,0:T(8,128)(2,1)S(1)}, bf16[96,2048]{1,0:T(8,128)(2,1)S(1)}, u32[]{:S(2)}, u32[]{:S(2)}) %collective-permute-start.10) | collective-permute-done | bytes 393248 | tf_op jit(solution)/shard_map/ppermute | solution.py:24
  164.4 6.5 %collective-permute-done.11.refs_7_ = bf16[96,2048]{1,0:T(8,128)(2,1)S(1)} collective-permute-done((bf16[96,2048]{1,0:T(8,128)(2,1)S(1)}, bf16[96,2048]{1,0:T(8,128)(2,1)S(1)}, u32[]{:S(2)}, u32[]{:S(2)}) %collective-permute-start.11) | collective-permute-done | bytes 393248 | tf_op jit(solution)/shard_map/ppermute | solution.py:24
  181.6 5.2 %collective-permute-done.7.refs_3_ = bf16[96,2048]{1,0:T(8,128)(2,1)} collective-permute-done((bf16[96,2048]{1,0:T(8,128)(2,1)S(1)}, bf16[96,2048]{1,0:T(8,128)(2,1)}, u32[]{:S(2)}, u32[]{:S(2)}) %collective-permute-start.7) | collective-permute-done | bytes 393248 | tf_op jit(solution)/shard_map/ppermute | solution.py:24
  192.8 7.5 %collective-permute-done.15.refs_11_ = bf16[96,2048]{1,0:T(8,128)(2,1)S(1)} collective-permute-done((bf16[96,2048]{1,0:T(8,128)(2,1)S(1)}, bf16[96,2048]{1,0:T(8,128)(2,1)S(1)}, u32[]{:S(2)}, u32[]{:S(2)}) %collective-permute-start.15) | collective-permute-done | bytes 393248 | tf_op jit(solution)/shard_map/ppermute | solution.py:28
  211.9 4.2 %collective-permute-done.9.refs_5_ = bf16[96,2048]{1,0:T(8,128)(2,1)} collective-permute-done((bf16[96,2048]{1,0:T(8,128)(2,1)}, bf16[96,2048]{1,0:T(8,128)(2,1)}, u32[]{:S(2)}, u32[]{:S(2)}) %collective-permute-start.9) | collective-permute-done | bytes 393248 | tf_op jit(solution)/shard_map/ppermute | solution.py:24
  216.1 5.1 %collective-permute-start.32 = (bf16[4,2,256,128]{3,2,1,0:T(8,128)(2,1)}, bf16[4,2,256,128]{3,2,1,0:T(8,128)(2,1)}, u32[]{:S(2)}, u32[]{:S(2)}) collective-permute-start(bf16[4,2,256,128]{3,2,1,0:T(8,128)(2,1)} %pad_maximum_fusion.4.refs_0_), channel_id=1, source_target_pairs={{0,64},{32,96},{64,0},{96,32},{1,65},{33,97},{65,1},{97,33},{2,66}... | collective-permute-start | bytes 1572872 | tf_op jit(solution)/shard_map/ppermute | solution.py:24
  226.8 16.2 %hidden.3.refs_1_.refs_0_ = bf16[576,1024]{1,0:T(8,128)(2,1)S(1)} custom-call(bf16[96,2048]{1,0:T(8,128)(2,1)S(1)} %collective-permute-done.4.refs_0_, bf16[96,2048]{1,0:T(8,128)(2,1)S(1)} %copy-done.4, bf16[96,2048]{1,0:T(8,128)(2,1)S(1)} %copy-done.2, bf16[96,2048]{1,0:T(8,128)(2,1)} %collective-permute-done.7.refs_3_, bf16[96,2048]{1,0:T(8,128)(2,1)S(1)} %copy-done.6, ...), custom_call_target="tpu_custom_call" | custom-call | flops 9663676416 | bytes 21495808 | tf_op jit(solution)/shard_map/hidden/pallas_call | solution.py:277
  243.0 4.8 %down.3 = (bf16[96,2048]{1,0:T(8,128)(2,1)S(1)}, bf16[96,2048]{1,0:T(8,128)(2,1)S(1)}, bf16[96,2048]{1,0:T(8,128)(2,1)S(1)}, bf16[96,2048]{1,0:T(8,128)(2,1)S(1)}) custom-call(bf16[576,1024]{1,0:T(8,128)(2,1)S(1)} %hidden.3.refs_1_.refs_0_, bf16[1,512,4096]{2,1,0:T(8,128)(2,1)S(1)} %copy-done, bf16[1,512,4096]{2,1,0:T(8,128)(2,1)} %collective-permute-done.16.refs_3_.refs_2_), custom_call_target="tpu_custom_call" | custom-call | flops 1610612736 | bytes 10354688 | tf_op jit(solution)/shard_map/down/pallas_call | solution.py:325
  249.9 10.6 %hidden.2.refs_0_ = bf16[192,1024]{1,0:T(8,128)(2,1)S(1)} custom-call(bf16[96,2048]{1,0:T(8,128)(2,1)S(1)} %reshape.337.refs_0_, bf16[96,2048]{1,0:T(8,128)(2,1)S(1)} %collective-permute-done.refs_1_, bf16[96,2048]{1,0:T(8,128)(2,1)S(1)} %reshape.338.refs_2_, bf16[96,2048]{1,0:T(8,128)(2,1)S(1)} %collective-permute-done.1.refs_3_, ...), custom_call_target="tpu_custom_call" | custom-call | flops 3221225472 | bytes 18350080 | tf_op jit(solution)/shard_map/hidden/pallas_call | solution.py:277
  260.6 8.1 %down.2 = (bf16[192,2048]{1,0:T(8,128)(2,1)S(1)}, bf16[96,2048]{1,0:T(8,128)(2,1)S(1)}, bf16[96,2048]{1,0:T(8,128)(2,1)S(1)}, bf16[96,2048]{1,0:T(8,128)(2,1)S(1...) custom-call(bf16[192,1024]{1,0:T(8,128)(2,1)S(1)} %hidden.2.refs_0_,, ...), custom_call_target="tpu_custom_call" | custom-call | flops 4831838208 | bytes 14286848 | tf_op jit(solution)/shard_map/down/pallas_call | solution.py:325
  273.9 9.8 %collective-permute-done.19 = bf16[96,2048]{1,0:T(8,128)(2,1)S(1)} collective-permute-done((bf16[96,2048]{1,0:T(8,128)(2,1)S(1)}, bf16[96,2048]{1,0:T(8,128)(2,1)S(1)}, u32[]{:S(2)}, u32[]{:S(2)}) %collective-permute-start.19) | collective-permute-done | bytes 393248 | tf_op jit(solution)/shard_map/ppermute | solution.py:24
  287.7 4.4 %collective-permute-done.27 = bf16[96,1024]{1,0:T(8,128)(2,1)S(1)} collective-permute-done((bf16[96,1024]{1,0:T(8,128)(2,1)S(1)}, bf16[96,1024]{1,0:T(8,128)(2,1)S(1)}, u32[]{:S(2)}, u32[]{:S(2)}) %collective-permute-start.27) | collective-permute-done | bytes 196640 | tf_op jit(solution)/shard_map/ppermute | solution.py:24
  294.6 8.6 %collective-permute-done.20 = bf16[192,2048]{1,0:T(8,128)(2,1)S(1)} collective-permute-done((bf16[192,2048]{1,0:T(8,128)(2,1)S(1)}, bf16[192,2048]{1,0:T(8,128)(2,1)S(1)}, u32[]{:S(2)}, u32[]{:S(2)}) %collective-permute-start.20) | collective-permute-done | bytes 786464 | tf_op jit(solution)/shard_map/ppermute | solution.py:24
  303.2 5.4 %collective-permute-done.18 = bf16[192,2048]{1,0:T(8,128)(2,1)S(1)} collective-permute-done((bf16[192,2048]{1,0:T(8,128)(2,1)S(1)}, bf16[192,2048]{1,0:T(8,128)(2,1)S(1)}, u32[]{:S(2)}, u32[]{:S(2)}) %collective-permute-start.18) | collective-permute-done | bytes 786464 | tf_op jit(solution)/shard_map/ppermute | solution.py:24
  318.0 6.9 %collective-permute-done.21 = bf16[96,2048]{1,0:T(8,128)(2,1)} collective-permute-done((bf16[96,2048]{1,0:T(8,128)(2,1)S(1)}, bf16[96,2048]{1,0:T(8,128)(2,1)}, u32[]{:S(2)}, u32[]{:S(2)}) %collective-permute-start.21) | collective-permute-done | bytes 393248 | tf_op jit(solution)/shard_map/ppermute | solution.py:28
  328.0 4.9 %all-to-all-start.3 = ((bf16[8,24,2048]{2,1,0:T(8,128)(2,1)}), bf16[8,24,2048]{2,1,0:T(8,128)(2,1)S(1)}, u32[]{:S(2)}, u32[]{:S(2)}) async-start(bf16[8,24,2048]{2,1,0:T(8,128)(2,1)} %copy.88), calls=%async_computation.3 | async-start | bytes 1572864 | tf_op jit(solution)/shard_map/all_to_all | solution.py:502
  (187 shorter events, 102.2 us)
Async XLA Ops:
  6.3 59.9 %all-to-all-start = ((bf16[16,2,512,128]{3,2,1,0:T(8,128)(2,1)}), bf16[16,2,512,128]{3,2,1,0:T(8,128)(2,1)}, u32[]{:S(2)}, u32[]{:S(2)}) async-start(bf16[16,2,512,128]{3,2,1,0:T(8,128)(2,1)} %select.152), calls=%async_computation | async-start | bytes 8388608 | tf_op jit(solution)/shard_map/all_to_all | solution.py:380
  88.5 30.3 %all-to-all-start.1 = ((bf16[8,32,4096]{2,1,0:T(8,128)(2,1)}), bf16[8,32,4096]{2,1,0:T(8,128)(2,1)S(1)}, u32[]{:S(2)}, u32[]{:S(2)}) async-start(bf16[8,32,4096]{2,1,0:T(8,128)(2,1)} %bitcast.50), calls=%async_computation.1 | async-start | bytes 4194304 | tf_op jit(solution)/shard_map/all_to_all | solution.py:400
  94.8 126.4 %collective-permute-start.2 = (bf16[1,512,4096]{2,1,0:T(8,128)(2,1)}, bf16[1,512,4096]{2,1,0:T(8,128)(2,1)}, u32[]{:S(2)}, u32[]{:S(2)}) collective-permute-start(bf16[1,512,4096]{2,1,0:T(8,128)(2,1)} %refs_12_.1), channel_id=1, source_target_pairs={{0,8},{8,0},{1,9},{9,1},{2,10},{10,2},{3,11},{11,3},{4,12},{12,4},... | collective-permute-start | bytes 12582920 | tf_op jit(solution)/shard_map/ppermute | solution.py:28
  94.9 127.9 %collective-permute-start.3 = (bf16[1,512,4096]{2,1,0:T(8,128)(2,1)}, bf16[1,512,4096]{2,1,0:T(8,128)(2,1)}, u32[]{:S(2)}, u32[]{:S(2)}) collective-permute-start(bf16[1,512,4096]{2,1,0:T(8,128)(2,1)} %refs_13_.1), channel_id=1, source_target_pairs={{0,8},{8,0},{1,9},{9,1},{2,10},{10,2},{3,11},{11,3},{4,12},{12,4},... | collective-permute-start | bytes 12582920 | tf_op jit(solution)/shard_map/ppermute | solution.py:28
  121.3 15.8 %all-to-all-start.2 = ((bf16[8,24,2048]{2,1,0:T(8,128)(2,1)}), bf16[8,24,2048]{2,1,0:T(8,128)(2,1)S(1)}, u32[]{:S(2)}, u32[]{:S(2)}) async-start(bf16[8,24,2048]{2,1,0:T(8,128)(2,1)} %bitcast.12), calls=%async_computation.2 | async-start | bytes 1572864 | tf_op jit(solution)/shard_map/all_to_all | solution.py:424
  126.4 16.4 %collective-permute-start.30 = (bf16[2,2,256,128]{3,2,1,0:T(8,128)(2,1)S(1)}, bf16[2,2,256,128]{3,2,1,0:T(8,128)(2,1)S(1)}, u32[]{:S(2)}, u32[]{:S(2)}) collective-permute-start(bf16[2,2,256,128]{3,2,1,0:T(8,128)(2,1)S(1)} %pad_maximum_fusion.8), channel_id=1, source_target_pairs={{0,16},{16,0},{1,17},{17,1},{2,18},{18,2},{3,19},{19,3},{4,20},{20... | collective-permute-start | bytes 786440 | tf_op jit(solution)/shard_map/ppermute | solution.py:28
  128.5 114.5 %collective-permute-start.16 = (bf16[1,512,4096]{2,1,0:T(8,128)(2,1)}, bf16[1,512,4096]{2,1,0:T(8,128)(2,1)}, u32[]{:S(2)}, u32[]{:S(2)}) collective-permute-start(bf16[1,512,4096]{2,1,0:T(8,128)(2,1)} %refs_1_.1), channel_id=1, source_target_pairs={{0,8},{8,0},{1,9},{9,1},{2,10},{10,2},{3,11},{11,3},{4,12},{12,4},... | collective-permute-start | bytes 12582920 | tf_op jit(solution)/shard_map/ppermute | solution.py:28
  137.4 12.8 %collective-permute-start = (bf16[96,2048]{1,0:T(8,128)(2,1)S(1)}, bf16[96,2048]{1,0:T(8,128)(2,1)S(1)}, u32[]{:S(2)}, u32[]{:S(2)}) collective-permute-start(bf16[96,2048]{1,0:T(8,128)(2,1)S(1)} %reshape.337.refs_0_), channel_id=1, source_target_pairs={{0,16},{16,0},{1,17},{17,1},{2,18},{18,2},{3,19},{19,3},{4,20},{20... | collective-permute-start | bytes 1179656 | tf_op jit(solution)/shard_map/ppermute | solution.py:28
  186.8 13.5 %collective-permute-start.15 = (bf16[96,2048]{1,0:T(8,128)(2,1)S(1)}, bf16[96,2048]{1,0:T(8,128)(2,1)S(1)}, u32[]{:S(2)}, u32[]{:S(2)}) collective-permute-start(bf16[96,2048]{1,0:T(8,128)(2,1)S(1)} %pad_maximum_fusion.5), channel_id=1, source_target_pairs={{0,16},{16,0},{1,17},{17,1},{2,18},{18,2},{3,19},{19,3},{4,20},{20... | collective-permute-start | bytes 1179656 | tf_op jit(solution)/shard_map/ppermute | solution.py:28
  191.3 24.9 %collective-permute-start.12 = (bf16[192,2048]{1,0:T(8,128)(2,1)}, bf16[192,2048]{1,0:T(8,128)(2,1)S(1)}, u32[]{:S(2)}, u32[]{:S(2)}) collective-permute-start(bf16[192,2048]{1,0:T(8,128)(2,1)} %pad_maximum_fusion.1), channel_id=1, source_target_pairs={{0,16},{16,0},{1,17},{17,1},{2,18},{18,2},{3,19},{19,3},{4,20},{20... | collective-permute-start | bytes 2359304 | tf_op jit(solution)/shard_map/ppermute | solution.py:28
  201.1 15.1 %collective-permute-start.9 = (bf16[96,2048]{1,0:T(8,128)(2,1)}, bf16[96,2048]{1,0:T(8,128)(2,1)}, u32[]{:S(2)}, u32[]{:S(2)}) collective-permute-start(bf16[96,2048]{1,0:T(8,128)(2,1)} %collective-permute-done.7.refs_3_), channel_id=1, source_target_pairs={{0,96},{32,0},{64,32},{96,64},{1,97},{33,1},{65,33},{97,65},{2,98}... | collective-permute-start | bytes 1179656 | tf_op jit(solution)/shard_map/ppermute | solution.py:24
  216.1 117.9 %collective-permute-start.31 = (bf16[4,2,256,128]{3,2,1,0:T(8,128)(2,1)}, bf16[4,2,256,128]{3,2,1,0:T(8,128)(2,1)}, u32[]{:S(2)}, u32[]{:S(2)}) collective-permute-start(bf16[4,2,256,128]{3,2,1,0:T(8,128)(2,1)} %pad_maximum_fusion.4.refs_0_), channel_id=1, source_target_pairs={{0,32},{32,64},{64,96},{96,0},{1,33},{33,65},{65,97},{97,1},{2,34}... | collective-permute-start | bytes 1572872 | tf_op jit(solution)/shard_map/ppermute | solution.py:24
  216.1 117.9 %collective-permute-start.32 = (bf16[4,2,256,128]{3,2,1,0:T(8,128)(2,1)}, bf16[4,2,256,128]{3,2,1,0:T(8,128)(2,1)}, u32[]{:S(2)}, u32[]{:S(2)}) collective-permute-start(bf16[4,2,256,128]{3,2,1,0:T(8,128)(2,1)} %pad_maximum_fusion.4.refs_0_), channel_id=1, source_target_pairs={{0,64},{32,96},{64,0},{96,32},{1,65},{33,97},{65,1},{97,33},{2,66}... | collective-permute-start | bytes 1572872 | tf_op jit(solution)/shard_map/ppermute | solution.py:24
  221.2 28.7 %collective-permute-start.1 = (bf16[96,2048]{1,0:T(8,128)(2,1)S(1)}, bf16[96,2048]{1,0:T(8,128)(2,1)S(1)}, u32[]{:S(2)}, u32[]{:S(2)}) collective-permute-start(bf16[96,2048]{1,0:T(8,128)(2,1)S(1)} %reshape.338.refs_2_), channel_id=1, source_target_pairs={{0,16},{16,0},{1,17},{17,1},{2,18},{18,2},{3,19},{19,3},{4,20},{20... | collective-permute-start | bytes 1179656 | tf_op jit(solution)/shard_map/ppermute | solution.py:28
  247.8 22.7 %collective-permute-start.24 = (bf16[96,2048]{1,0:T(8,128)(2,1)S(1)}, bf16[96,2048]{1,0:T(8,128)(2,1)S(1)}, u32[]{:S(2)}, u32[]{:S(2)}) collective-permute-start(bf16[96,2048]{1,0:T(8,128)(2,1)S(1)} %get-tuple-element.39), channel_id=1, source_target_pairs={{0,16},{16,0},{1,17},{17,1},{2,18},{18,2},{3,19},{19,3},{4,20},{20... | collective-permute-start | bytes 1179656 | tf_op jit(solution)/shard_map/ppermute | solution.py:28
  268.7 18.7 %collective-permute-start.23 = (bf16[192,2048]{1,0:T(8,128)(2,1)S(1)}, bf16[192,2048]{1,0:T(8,128)(2,1)S(1)}, u32[]{:S(2)}, u32[]{:S(2)}) collective-permute-start(bf16[192,2048]{1,0:T(8,128)(2,1)S(1)} %get-tuple-element.37), channel_id=1, source_target_pairs={{0,16},{16,0},{1,17},{17,1},{2,18},{18,2},{3,19},{19,3},{4,20},{20... | collective-permute-start | bytes 2359304 | tf_op jit(solution)/shard_map/ppermute | solution.py:28
  270.5 13.2 %collective-permute-start.19 = (bf16[96,2048]{1,0:T(8,128)(2,1)S(1)}, bf16[96,2048]{1,0:T(8,128)(2,1)S(1)}, u32[]{:S(2)}, u32[]{:S(2)}) collective-permute-start(bf16[96,2048]{1,0:T(8,128)(2,1)S(1)} %get-tuple-element.33), channel_id=1, source_target_pairs={{0,32},{32,64},{64,96},{96,0},{1,33},{33,65},{65,97},{97,1},{2,34}... | collective-permute-start | bytes 1179656 | tf_op jit(solution)/shard_map/ppermute | solution.py:24
  270.5 13.4 %collective-permute-start.17 = (bf16[96,2048]{1,0:T(8,128)(2,1)S(1)}, bf16[96,2048]{1,0:T(8,128)(2,1)S(1)}, u32[]{:S(2)}, u32[]{:S(2)}) collective-permute-start(bf16[96,2048]{1,0:T(8,128)(2,1)S(1)} %get-tuple-element.29), channel_id=1, source_target_pairs={{0,96},{32,0},{64,32},{96,64},{1,97},{33,1},{65,33},{97,65},{2,98}... | collective-permute-start | bytes 1179656 | tf_op jit(solution)/shard_map/ppermute | solution.py:24
  287.4 15.8 %collective-permute-start.20 = (bf16[192,2048]{1,0:T(8,128)(2,1)S(1)}, bf16[192,2048]{1,0:T(8,128)(2,1)S(1)}, u32[]{:S(2)}, u32[]{:S(2)}) collective-permute-start(bf16[192,2048]{1,0:T(8,128)(2,1)S(1)} %pad_maximum_fusion.3), channel_id=1, source_target_pairs={{0,32},{32,64},{64,96},{96,0},{1,33},{33,65},{65,97},{97,1},{2,34}... | collective-permute-start | bytes 2359304 | tf_op jit(solution)/shard_map/ppermute | solution.py:24
  292.1 16.6 %collective-permute-start.18 = (bf16[192,2048]{1,0:T(8,128)(2,1)S(1)}, bf16[192,2048]{1,0:T(8,128)(2,1)S(1)}, u32[]{:S(2)}, u32[]{:S(2)}) collective-permute-start(bf16[192,2048]{1,0:T(8,128)(2,1)S(1)} %pad_maximum_fusion.2), channel_id=1, source_target_pairs={{0,96},{32,0},{64,32},{96,64},{1,97},{33,1},{65,33},{97,65},{2,98}... | collective-permute-start | bytes 2359304 | tf_op jit(solution)/shard_map/ppermute | solution.py:24
  292.4 20.3 %collective-permute-start.22 = (bf16[96,2048]{1,0:T(8,128)(2,1)S(1)}, bf16[96,2048]{1,0:T(8,128)(2,1)S(1)}, u32[]{:S(2)}, u32[]{:S(2)}) collective-permute-start(bf16[96,2048]{1,0:T(8,128)(2,1)S(1)} %get-tuple-element.35), channel_id=1, source_target_pairs={{0,16},{16,0},{1,17},{17,1},{2,18},{18,2},{3,19},{19,3},{4,20},{20... | collective-permute-start | bytes 1179656 | tf_op jit(solution)/shard_map/ppermute | solution.py:28
  312.8 21.2 %collective-permute-start.33 = (bf16[4,2,256,128]{3,2,1,0:T(8,128)(2,1)}, bf16[4,2,256,128]{3,2,1,0:T(8,128)(2,1)S(1)}, u32[]{:S(2)}, u32[]{:S(2)}) collective-permute-start(bf16[4,2,256,128]{3,2,1,0:T(8,128)(2,1)} %pad_maximum_fusion.4.refs_0_), channel_id=1, source_target_pairs={{0,96},{32,0},{64,32},{96,64},{1,97},{33,1},{65,33},{97,65},{2,98}... | collective-permute-start | bytes 1572872 | tf_op jit(solution)/shard_map/ppermute | solution.py:24
  312.9 12.0 %collective-permute-start.21 = (bf16[96,2048]{1,0:T(8,128)(2,1)S(1)}, bf16[96,2048]{1,0:T(8,128)(2,1)}, u32[]{:S(2)}, u32[]{:S(2)}) collective-permute-start(bf16[96,2048]{1,0:T(8,128)(2,1)S(1)} %slice.116), channel_id=1, source_target_pairs={{0,16},{16,0},{1,17},{17,1},{2,18},{18,2},{3,19},{19,3},{4,20},{20... | collective-permute-start | bytes 1179656 | tf_op jit(solution)/shard_map/ppermute | solution.py:28
  328.0 14.3 %all-to-all-start.3 = ((bf16[8,24,2048]{2,1,0:T(8,128)(2,1)}), bf16[8,24,2048]{2,1,0:T(8,128)(2,1)S(1)}, u32[]{:S(2)}, u32[]{:S(2)}) async-start(bf16[8,24,2048]{2,1,0:T(8,128)(2,1)} %copy.88), calls=%async_computation.3 | async-start | bytes 1572864 | tf_op jit(solution)/shard_map/all_to_all | solution.py:502
  (39 other events, 328.8 us)
